TPU v7x, 32 devices: a whole 2x2x4 slice. The times are simulated.
32 devices in a mesh: dp: 8 (over y, x, core), tensor: 4 (over z).
Axes of the slice: x: 2, y: 2, z: 4, core: 2. Of those that a mesh axis runs over, the one named last changes fastest.
Arguments:
- tokens: bfloat16 [16384, 768], P(('dp', 'tensor')), may hold values from -6 to 6
- starts: int32 [8, 8], P('dp'), may hold values from 0 to 2047, as said below
- w_qkv: bfloat16 [768, 2304], P(None, 'tensor'), may hold values from -0.21875 to 0.21875
- b_qkv: bfloat16 [2304], P('tensor'), may hold values from -3 to 3
- w_out: bfloat16 [768, 768], P('tensor'), may hold values from -2 to 2
- b_out: bfloat16 [768], replicated, may hold values from -3 to 3
- gain_one: bfloat16 [768], replicated, may hold values from 0.099609375 to 1.8984375
- shift_one: bfloat16 [768], replicated, may hold values from -3 to 3
- w_in: bfloat16 [768, 3072], P(None, 'tensor'), may hold values from -0.21875 to 0.21875
- b_in: bfloat16 [3072], P('tensor'), may hold values from -3 to 3
- w_two: bfloat16 [3072, 768], P('tensor'), may hold values from -0.21875 to 0.21875
- b_two: bfloat16 [768], replicated, may hold values from -3 to 3
- gain_two: bfloat16 [768], replicated, may hold values from 0.099609375 to 1.8984375
- shift_two: bfloat16 [768], replicated, may hold values from -3 to 3
- cotangent: bfloat16 [16384, 768], P(('dp', 'tensor')), may hold values from -6 to 6
Outputs:
- block_out: bfloat16 [16384, 768], P(('dp', 'tensor'))
- d_tokens: bfloat16 [16384, 768], P(('dp', 'tensor'))
- d_w_qkv: float32 [768, 2304], P(None, 'tensor')
- d_b_qkv: float32 [2304], P('tensor')
- d_w_out: float32 [768, 768], P('tensor')
- d_b_out: float32 [768], replicated
- d_gain_one: float32 [768], replicated
- d_shift_one: float32 [768], replicated
- d_w_in: float32 [768, 3072], P(None, 'tensor')
- d_b_in: float32 [3072], P('tensor')
- d_w_two: float32 [3072, 768], P('tensor')
- d_b_two: float32 [768], replicated
- d_gain_two: float32 [768], replicated
- d_shift_two: float32 [768], replicated
Inputs may be any that keep to these rules, and one draw needn't show every extreme that they name: Each row holds exactly 8 documents: its first start is 0 and its starts rise strictly. In the first row the last document is a single token.
All inputs are finite; a program needn't handle non-finite values.
Results may differ from a plain program's by a relative error of at most 0.014.
Values may be sent and summed in bfloat16 or wider, within the bound.
No kernel may reach another device: no remote copies, remote signals or barrier semaphores. Data moves between devices by JAX's collectives and lax.ppermute only.
A program may use at most 192 MiB of HBM per device.

v0:
```python
import math

import jax
import jax.numpy as jnp
from jax import lax
from jax.sharding import PartitionSpec as P

HEAD = 64
GROUP = 64
ROW_LEN = 2048
DOCS = 8


highest = lax.Precision.HIGHEST


def doc_tables(starts_row):
    places = jnp.arange(ROW_LEN, dtype=jnp.int32)
    started = (places[:, None] >= starts_row[None, :]).astype(jnp.int32)
    doc_ids = jnp.sum(started, axis=1) - 1
    onehot = (doc_ids[:, None] == jnp.arange(DOCS, dtype=jnp.int32)[None, :]).astype(jnp.int32)
    finish = jnp.concatenate([starts_row[1:], jnp.full((1,), ROW_LEN, jnp.int32)])
    own_start = jnp.sum(onehot * starts_row[None, :], axis=1)
    own_len = jnp.sum(onehot * (finish - starts_row)[None, :], axis=1)
    angles = 0.5 * math.pi * (places - own_start).astype(jnp.float32) / own_len.astype(jnp.float32)
    return (angles, doc_ids)


def attend(mixed, angles, doc_ids):
    length = mixed.shape[0]
    head_count = mixed.shape[1] // (3 * HEAD)
    blocks = length // GROUP
    pieces = mixed.reshape(blocks, GROUP, head_count, 3, HEAD)
    queries = jax.nn.relu(pieces[:, :, :, 0])
    key_pos = jax.nn.relu(pieces[:, :, :, 1])
    values = pieces[:, :, :, 2]
    cosine = jnp.cos(angles).reshape(blocks, GROUP, 1, 1)
    sines = jnp.sin(angles).reshape(blocks, GROUP, 1, 1)
    query_feat = jnp.concatenate([queries * cosine, queries * sines], axis=-1)
    key_feat = jnp.concatenate([key_pos * cosine, key_pos * sines], axis=-1)
    doc_blocks = doc_ids.reshape(blocks, GROUP)
    within = jnp.arange(GROUP, dtype=jnp.int32)
    inside_mask = (
        (doc_blocks[:, :, None] == doc_blocks[:, None, :])
        & (within[None, :, None] >= within[None, None, :])
    ).astype(jnp.float32)
    scores = (
        jnp.einsum("bihf,bjhf->bhij", query_feat, key_feat, precision=highest)
        * inside_mask[:, None]
    )
    numerator = jnp.einsum("bhij,bjhd->bihd", scores, values, precision=highest)
    denominator = jnp.transpose(jnp.sum(scores, axis=-1), (0, 2, 1))
    first_doc = doc_blocks[:, 0]
    last_doc = doc_blocks[:, -1]
    tail_mask = (doc_blocks == last_doc[:, None]).astype(jnp.float32)
    states = jnp.einsum("bjhf,bjhd,bj->bhfd", key_feat, values, tail_mask, precision=highest)
    key_sums = jnp.einsum("bjhf,bj->bhf", key_feat, tail_mask, precision=highest)
    order = jnp.arange(blocks, dtype=jnp.int32)
    link_mask = (
        (last_doc[None, :] == first_doc[:, None]) & (order[None, :] < order[:, None])
    ).astype(jnp.float32)
    carried = jnp.einsum("cb,bhfd->chfd", link_mask, states, precision=highest)
    carried_sum = jnp.einsum("cb,bhf->chf", link_mask, key_sums, precision=highest)
    opening = (doc_blocks == first_doc[:, None]).astype(jnp.float32)
    numerator = numerator + jnp.einsum(
        "bihf,bhfd,bi->bihd", query_feat, carried, opening, precision=highest
    )
    denominator = denominator + jnp.einsum(
        "bihf,bhf,bi->bih", query_feat, carried_sum, opening, precision=highest
    )
    result = numerator / jnp.maximum(denominator, 1.0)[..., None]
    return result.reshape(length, head_count * HEAD)


def attend_rows(mixed, angles, doc_ids):
    row_count = angles.shape[0]
    shaped = mixed.reshape(row_count, angles.shape[1], mixed.shape[1])
    return jax.vmap(attend)(shaped, angles, doc_ids).reshape(mixed.shape[0], -1)


def normalize(rows_in, gain, shift):
    centred = rows_in - jnp.mean(rows_in, axis=-1, keepdims=True)
    spread = jnp.mean(centred * centred, axis=-1, keepdims=True)
    return centred * lax.rsqrt(spread + 1e-05) * gain + shift


def smooth(values):
    return jax.nn.gelu(values)


def inner_rows(left, right):
    return lax.dot_general(
        left, right, (((0,), (0,)), ((), ())), preferred_element_type=jnp.float32
    )


def times_rows(left, right):
    return lax.dot_general(
        left, right, (((1,), (1,)), ((), ())), preferred_element_type=jnp.float32
    )


def rows_product(source, weight):
    return jnp.dot(source, weight, preferred_element_type=jnp.float32)


def rows_back(source, weight):
    return times_rows(source, weight)


def on_device(
    tokens,
    starts,
    w_qkv,
    b_qkv,
    w_out,
    b_out,
    gain_one,
    shift_one,
    w_in,
    b_in,
    w_two,
    b_two,
    gain_two,
    shift_two,
    cotangent,
):
    angles, doc_ids = jax.vmap(doc_tables)(starts)
    bias_qkv = b_qkv.astype(jnp.float32)
    bias_in = b_in.astype(jnp.float32)
    gain_a = gain_one.astype(jnp.float32)
    shift_a = shift_one.astype(jnp.float32)
    gain_b = gain_two.astype(jnp.float32)
    shift_b = shift_two.astype(jnp.float32)
    input_full = lax.all_gather(tokens, "tensor", axis=0, tiled=True)
    mixed = jnp.dot(input_full, w_qkv, preferred_element_type=jnp.float32) + bias_qkv
    attended = attend_rows(mixed, angles, doc_ids).astype(jnp.bfloat16)
    branch = lax.psum_scatter(
        rows_product(attended, w_out), "tensor", scatter_dimension=0, tiled=True
    ) + b_out.astype(jnp.float32)
    first_sum = tokens.astype(jnp.float32) + branch
    first_low = normalize(first_sum, gain_a, shift_a).astype(jnp.bfloat16)
    middle_full = lax.all_gather(first_low, "tensor", axis=0, tiled=True)
    hidden = jnp.dot(middle_full, w_in, preferred_element_type=jnp.float32) + bias_in
    active = smooth(hidden).astype(jnp.bfloat16)
    second = lax.psum_scatter(
        rows_product(active, w_two), "tensor", scatter_dimension=0, tiled=True
    ) + b_two.astype(jnp.float32)
    second_sum = first_low.astype(jnp.float32) + second
    block_out = normalize(second_sum, gain_b, shift_b).astype(jnp.bfloat16)
    input_back = lax.all_gather(tokens, "tensor", axis=0, tiled=True)
    middle_back = lax.all_gather(first_low, "tensor", axis=0, tiled=True)
    unused_two, norm_two_back = jax.vjp(normalize, second_sum, gain_b, shift_b)
    d_r2, d_gain_two, d_shift_two = norm_two_back(cotangent.astype(jnp.float32))
    d_second = d_r2.astype(jnp.bfloat16)
    d_b_two = jnp.sum(d_second, axis=0, dtype=jnp.float32)
    second_full = lax.all_gather(d_second, "tensor", axis=0, tiled=True)
    hidden_again = jnp.dot(middle_back, w_in, preferred_element_type=jnp.float32) + bias_in
    active_val, gelu_back = jax.vjp(smooth, hidden_again)
    active_again = active_val.astype(jnp.bfloat16)
    d_w_two = inner_rows(active_again, second_full)
    d_active = times_rows(second_full, w_two)
    d_hidden = gelu_back(d_active)[0].astype(jnp.bfloat16)
    d_b_in = jnp.sum(d_hidden, axis=0, dtype=jnp.float32)
    d_w_in = inner_rows(middle_back, d_hidden)
    d_first = (
        lax.psum_scatter(rows_back(d_hidden, w_in), "tensor", scatter_dimension=0, tiled=True)
        + d_r2
    )
    unused_one, norm_one_back = jax.vjp(normalize, first_sum, gain_a, shift_a)
    d_r1, d_gain_one, d_shift_one = norm_one_back(d_first)
    d_branch = d_r1.astype(jnp.bfloat16)
    d_b_out = jnp.sum(d_branch, axis=0, dtype=jnp.float32)
    branch_full = lax.all_gather(d_branch, "tensor", axis=0, tiled=True)
    mixed_again = jnp.dot(input_back, w_qkv, preferred_element_type=jnp.float32) + bias_qkv
    attended_val, attend_back = jax.vjp(
        lambda mixed_in: attend_rows(mixed_in, angles, doc_ids), mixed_again
    )
    attended_again = attended_val.astype(jnp.bfloat16)
    d_w_out = inner_rows(attended_again, branch_full)
    d_attended = times_rows(branch_full, w_out)
    d_mixed = attend_back(d_attended)[0].astype(jnp.bfloat16)
    d_b_qkv = jnp.sum(d_mixed, axis=0, dtype=jnp.float32)
    d_w_qkv = inner_rows(input_back, d_mixed)
    d_tokens = (
        lax.psum_scatter(
            rows_back(d_mixed, w_qkv).astype(jnp.bfloat16),
            "tensor",
            scatter_dimension=0,
            tiled=True,
        ).astype(jnp.float32)
        + d_r1
    ).astype(jnp.bfloat16)
    d_w_qkv, d_b_qkv, d_w_out, d_w_in, d_b_in, d_w_two = lax.psum(
        (d_w_qkv, d_b_qkv, d_w_out, d_w_in, d_b_in, d_w_two), "dp"
    )
    d_b_out, d_gain_one, d_shift_one, d_b_two, d_gain_two, d_shift_two = lax.psum(
        (d_b_out, d_gain_one, d_shift_one, d_b_two, d_gain_two, d_shift_two), ("dp", "tensor")
    )
    return (
        block_out,
        d_tokens,
        d_w_qkv,
        d_b_qkv,
        d_w_out,
        d_b_out,
        d_gain_one,
        d_shift_one,
        d_w_in,
        d_b_in,
        d_w_two,
        d_b_two,
        d_gain_two,
        d_shift_two,
    )


def solution(mesh):
    in_specs = (
        P(("dp", "tensor"), None),
        P("dp", None),
        P(None, "tensor"),
        P("tensor"),
        P("tensor", None),
        P(),
        P(),
        P(),
        P(None, "tensor"),
        P("tensor"),
        P("tensor", None),
        P(),
        P(),
        P(),
        P(("dp", "tensor"), None),
    )
    out_specs = (
        P(("dp", "tensor"), None),
        P(("dp", "tensor"), None),
        P(None, "tensor"),
        P("tensor"),
        P("tensor", None),
        P(),
        P(),
        P(),
        P(None, "tensor"),
        P("tensor"),
        P("tensor", None),
        P(),
        P(),
        P(),
    )
    return jax.shard_map(
        on_device, mesh=mesh, in_specs=in_specs, out_specs=out_specs, check_vma=False
    )
```

profile of v0, /device:TPU:0, one launch (start us, length us, event | category | flops | bytes accessed | tf_op | source)
XLA Modules:
  0.0 1038.7 jit_solution(10530214980209661449)
XLA Ops:
  12.7 63.1 %all-gather.5.cloned.1.call-done = bf16[2048,768]{1,0:T(8,128)(2,1)} async-done(((bf16[512,768]{1,0:T(8,128)(2,1)}), bf16[2048,768]{1,0:T(8,128)(2,1)}) %all-gather.5.cloned.1.call-update) | async-done | bytes 3145744 | tf_op jit(solution)/shard_map/all_gather | solution.py:135
  75.8 6.3 convolution_add_fusion
  82.2 8.7 reshape_reshape.3
  90.9 8.2 fusion.101
  99.1 3.9 copy.193
  103.0 3.9 copy.191
  106.9 3.9 copy.192
  110.8 5.1 bitcast_multiply_fusion.4
  115.8 3.8 maximum_bitcast_fusion
  121.2 2.6 copy-done.6
  123.8 6.0 fusion.31
  129.9 4.1 fusion.28
  134.0 5.0 fusion.78
  139.0 5.4 multiply_reduce_fusion.1
  144.4 5.4 fusion.24
  150.5 9.1 divide_convert_fusion
  160.7 1.7 convert_element_type.153
  162.4 4.9 fusion.102
  169.7 107.1 %reduce-scatter.5.cloned.1.call-done = f32[512,768]{1,0:T(8,128)} async-done(((f32[2048,768]{1,0:T(8,128)}), f32[512,768]{1,0:T(8,128)}) %reduce-scatter.5.cloned.1.call-update) | async-done | bytes 1572880 | tf_op jit(solution)/shard_map/reduce_scatter | solution.py:138
  276.8 1.7 fusion.99
  280.2 64.1 %all-gather.7.cloned.1.call-done = bf16[2048,768]{1,0:T(8,128)(2,1)} async-done(((bf16[512,768]{1,0:T(8,128)(2,1)}), bf16[2048,768]{1,0:T(8,128)(2,1)}) %all-gather.7.cloned.1.call-update) | async-done | bytes 3145744 | tf_op jit(solution)/shard_map/all_gather | solution.py:143
  344.3 8.4 multiply_convert_fusion
  352.7 1.7 copy-done.88
  354.4 4.4 fusion.103
  361.3 107.1 %reduce-scatter.7.cloned.1.call-done = f32[512,768]{1,0:T(8,128)} async-done(((f32[2048,768]{1,0:T(8,128)}), f32[512,768]{1,0:T(8,128)}) %reduce-scatter.7.cloned.1.call-update) | async-done | bytes 1572880 | tf_op jit(solution)/shard_map/reduce_scatter | solution.py:146
  468.4 2.0 fusion.98
  474.7 1.7 convert_reduce_fusion.3
  476.5 64.1 %all-gather.9.cloned.1.call-done = bf16[2048,768]{1,0:T(8,128)(2,1)} async-done(((bf16[512,768]{1,0:T(8,128)(2,1)}), bf16[2048,768]{1,0:T(8,128)(2,1)}) %all-gather.9.cloned.1.call-update) | async-done | bytes 3145744 | tf_op jit(solution)/shard_map/all_gather | solution.py:157
  540.6 9.8 convert_reduce_fusion.1
  550.4 1.6 copy-done.89
  552.1 4.5 fusion.104
  556.7 109.5 %reduce-scatter.9.cloned.1.call-done = f32[512,768]{1,0:T(8,128)} async-done(((f32[2048,768]{1,0:T(8,128)}), f32[512,768]{1,0:T(8,128)}) %reduce-scatter.9.cloned.1.call-update) | async-done | bytes 1572880 | tf_op jit(solution)/shard_map/reduce_scatter | solution.py:167
  666.2 3.3 multiply_reduce_fusion.2
  671.3 1.7 convert_reduce_fusion.4
  673.7 63.5 %all-gather.11.cloned.1.call-done = bf16[2048,768]{1,0:T(8,128)(2,1)} async-done(((bf16[512,768]{1,0:T(8,128)(2,1)}), bf16[2048,768]{1,0:T(8,128)(2,1)}) %all-gather.11.cloned.1.call-update) | async-done | bytes 3145744 | tf_op jit(solution)/shard_map/all_gather | solution.py:174
  737.2 3.1 fusion.105
  740.3 2.6 reshape.798
  742.9 12.0 %fusion.21 = f32[32,3,64,64]{2,3,1,0:T(8,128)} fusion(f32[32,3,64,64]{2,3,1,0:T(8,128)} %copy-done.21, f32[32,64,64]{1,2,0:T(8,128)S(1)} %copy-done.12, f32[1,32,64,3,64]{2,1,4,3,0:T(8,128)} %reshape.798, f32[32,64,3]{1,2,0:T(4,128)S(1)} %copy-done.42), kind=kOutput, calls=%fused_computation.38 | convolution fusion | flops 302776320 | bytes 5267456 | tf_op jit(solution)/shard_map/transpose(jvp(vmap(bhij,bjhd->bihd)))/dot_general | solution.py:51
  754.9 7.4 fusion.19
  762.3 2.4 reshape.793
  764.7 5.4 multiply_reduce_fusion
  770.2 2.7 fusion.76
  773.2 4.0 copy.158
  777.2 8.3 fusion.42
  785.6 3.7 fusion.45
  789.3 5.8 fusion.30
  795.2 7.7 fusion.13
  802.9 7.0 fusion.38
  810.0 4.6 bitcast_add_fusion
  814.7 8.1 add_bitcast_fusion
  822.8 2.8 fusion.12
  825.6 2.8 convert_reduce_fusion
  828.5 7.4 copy.171
  835.9 6.7 convert_element_type.170
  842.5 4.1 convolution_convert_fusion
  847.0 7.1 fusion.108
  854.1 4.2 fusion.107
  858.3 1.6 fusion.106
  860.4 3.2 convolution_bitcast_fusion
  864.5 43.0 %all-reduce.3 = (f32[768]{0:T(1024)}, f32[768]{0:T(1024)}, f32[768]{0:T(1024)}, f32[768]{0:T(1024)}, f32[768]{0:T(1024)}, /*index=5*/f32[768]{0:T(1024)}) all-reduce(f32[768]{0:T(1024)S(1)} %copy-done.71, f32[768]{0:T(1024)S(1)} %copy-done.72, f32[768]{0:T(1024)S(1)} %copy-done.73, ...), channel_id=1, replica_groups=mesh['dp'=8,'tensor'=4] {'dp','tensor'}, use_global_device_ids=true, to_apply=%region_22.23 | all-reduce | flops 4608 | bytes 36864 | tf_op jit(solution)/shard_map/psum | solution.py:197
  907.5 14.0 %all-reduce.4 = (f32[576]{0:T(1024)}, f32[768]{0:T(1024)}) all-reduce(f32[576]{0:T(1024)S(1)} %reduce_sum.223, f32[768]{0:T(1024)S(1)} %copy-done.76), channel_id=1, replica_groups=mesh['dp'=8,'tensor'=4] {'dp'}, use_global_device_ids=true, to_apply=%region_19.20 | all-reduce | flops 1344 | bytes 10752 | tf_op jit(solution)/shard_map/psum | solution.py:194
  921.5 2.3 add_convert_fusion.1
  923.8 101.3 %all-reduce.8.cloned.1.call-done = (f32[768,576]{0,1:T(8,128)}, f32[192,768]{1,0:T(8,128)}, f32[768,768]{1,0:T(8,128)}, f32[768,768]{1,0:T(8,128)}) async-done(((f32[768,576]{0,1:T(8,128)}, f32[192,768]{1,0:T(8,128)}, f32[768,768]{1,0:T(8,128)}, f32[768,768]{1,0:T(8,128)}), (f32[768,576]{0,1:T(8,128)}, f32[192,768]{1,0:T(8,128)}, f32[768,768]{1,0:T(8,128)}, ...) | async-done | bytes 7077904 | tf_op jit(solution)/shard_map/psum | solution.py:194
  1025.1 2.9 copy.250
  (249 shorter events, 27.9 us)
Async XLA Ops:
  7.2 337.2 %copy-start = (bf16[768,768]{1,0:T(8,128)(2,1)S(1)}, bf16[768,768]{1,0:T(8,128)(2,1)}, u32[]{:S(2)}) copy-start(bf16[768,768]{1,0:T(8,128)(2,1)} %param.23) | copy-start | bytes 3538948
  7.2 68.6 %all-gather.5.cloned.1.call-start = ((), (), s32[]{:S(2)}) async-start(), calls=%async_computation.4 | async-start | bytes 3932160 | tf_op jit(solution)/shard_map/all_gather | solution.py:135
  7.9 268.9 %reduce-scatter.5.cloned.1.call-start = ((), (), s32[]{:S(2)}) async-start(), calls=%async_computation.5 | async-start | bytes 7864320 | tf_op jit(solution)/shard_map/reduce_scatter | solution.py:138
  12.1 117.7 %copy-start.61 = (s32[32]{0:T(128)}, s32[32]{0:T(128)S(1)}, u32[]{:S(2)}) copy-start(s32[32]{0:T(128)S(1)} %get-tuple-element.20) | copy-start | bytes 388
  12.1 117.7 %copy-start.64 = (s32[32]{0:T(128)}, s32[32]{0:T(128)S(1)}, u32[]{:S(2)}) copy-start(s32[32]{0:T(128)S(1)} %get-tuple-element.21) | copy-start | bytes 388
  12.2 109.0 %copy-start.39 = (f32[32,64]{1,0:T(8,128)}, f32[32,64]{1,0:T(8,128)S(1)}, u32[]{:S(2)}) copy-start(f32[32,64]{1,0:T(8,128)S(1)} %get-tuple-element.57) | copy-start | bytes 24580
  12.3 98.5 %copy-start.44 = (f32[32,64]{1,0:T(8,128)}, f32[32,64]{1,0:T(8,128)S(1)}, u32[]{:S(2)}) copy-start(f32[32,64]{1,0:T(8,128)S(1)} %get-tuple-element.71) | copy-start | bytes 24580
  12.3 98.4 %copy-start.46 = (f32[32,64]{1,0:T(8,128)}, f32[32,64]{1,0:T(8,128)S(1)}, u32[]{:S(2)}) copy-start(f32[32,64]{1,0:T(8,128)S(1)} %get-tuple-element.72) | copy-start | bytes 24580
  12.7 131.7 %copy-start.11 = (f32[32,64,64]{1,2,0:T(8,128)}, f32[32,64,64]{1,2,0:T(8,128)S(1)}, u32[]{:S(2)}) copy-start(f32[32,64,64]{1,2,0:T(8,128)S(1)} %and_convert_fusion) | copy-start | bytes 1572868
  119.6 19.4 %copy-start.4 = (f32[32,64,3,128]{3,1,2,0:T(8,128)}, f32[32,64,3,128]{3,1,2,0:T(8,128)S(1)}, u32[]{:S(2)}) copy-start(f32[32,64,3,128]{3,1,2,0:T(8,128)S(1)} %get-tuple-element.81) | copy-start | bytes 9437188
  119.6 30.9 %copy-start.2 = (f32[32,64,3,128]{3,1,2,0:T(8,128)}, f32[32,64,3,128]{3,1,2,0:T(8,128)S(1)}, u32[]{:S(2)}) copy-start(f32[32,64,3,128]{3,1,2,0:T(8,128)S(1)} %get-tuple-element.80) | copy-start | bytes 9437188
  121.2 12.8 %copy-start.35 = (f32[32,3,128]{2,0,1:T(8,128)}, f32[32,3,128]{2,0,1:T(8,128)S(1)}, u32[]{:S(2)}) copy-start(f32[32,3,128]{2,0,1:T(8,128)S(1)} %fusion.73) | copy-start | bytes 147460
  134.0 16.5 %copy-start.19 = (f32[32,3,128,64]{2,0,3,1:T(8,128)}, f32[32,3,128,64]{2,0,3,1:T(8,128)S(1)}, u32[]{:S(2)}) copy-start(f32[32,3,128,64]{2,0,3,1:T(8,128)S(1)} %fusion.28) | copy-start | bytes 9437188
  139.0 10.9 %copy-start.37 = (f32[32,3,1,64]{3,2,1,0:T(1,128)}, f32[32,3,1,64]{3,2,1,0:T(1,128)S(1)}, u32[]{:S(2)}) copy-start(f32[32,3,1,64]{3,2,1,0:T(1,128)S(1)} %fusion.78) | copy-start | bytes 73732
  144.4 5.5 copy-start.21
  144.4 5.5 copy-start.32
  150.5 9.1 copy-start.41
  162.4 4.9 copy-start.23
  167.2 109.6 %copy-start.27 = (bf16[512,768]{1,0:T(8,128)(2,1)S(1)}, bf16[512,768]{1,0:T(8,128)(2,1)}, u32[]{:S(2)}) copy-start(bf16[512,768]{1,0:T(8,128)(2,1)} %param.15) | copy-start | bytes 2359300
  167.3 177.1 %all-gather.7.cloned.1.call-start = ((), (), s32[]{:S(2)}) async-start(), calls=%async_computation.6 | async-start | bytes 3932160 | tf_op jit(solution)/shard_map/all_gather | solution.py:143
  278.6 74.1 %copy-start.50 = (f32[512]{0:T(512)}, f32[512]{0:T(512)S(1)}, u32[]{:S(2)}) copy-start(f32[512]{0:T(512)S(1)} %broadcast_multiply_fusion.1) | copy-start | bytes 6148
  278.9 73.8 %copy-start.57 = (f32[512]{0:T(512)}, f32[512]{0:T(512)S(1)}, u32[]{:S(2)}) copy-start(f32[512]{0:T(512)S(1)} %multiply_reduce_fusion.5) | copy-start | bytes 6148
  278.9 73.8 %copy-start.53 = (f32[512]{0:T(512)}, f32[512]{0:T(512)S(1)}, u32[]{:S(2)}) copy-start(f32[512]{0:T(512)S(1)} %fusion.86) | copy-start | bytes 6148
  280.2 188.3 %reduce-scatter.7.cloned.1.call-start = ((), (), s32[]{:S(2)}) async-start(), calls=%async_computation.7 | async-start | bytes 7864320 | tf_op jit(solution)/shard_map/reduce_scatter | solution.py:146
  280.2 72.5 %copy-start.74 = (f32[768]{0:T(1024)}, f32[768]{0:T(1024)S(1)}, u32[]{:S(2)}) copy-start(f32[768]{0:T(1024)S(1)} %convert_element_type.159) | copy-start | bytes 9220
  344.3 10.1 copy-start.86
  358.9 181.8 %all-gather.9.cloned.1.call-start = ((), (), s32[]{:S(2)}) async-start(), calls=%async_computation.8 | async-start | bytes 3932160 | tf_op jit(solution)/shard_map/all_gather | solution.py:157
  361.3 109.5 %copy-start.26 = (bf16[512,768]{1,0:T(8,128)(2,1)S(1)}, bf16[512,768]{1,0:T(8,128)(2,1)}, u32[]{:S(2)}) copy-start(bf16[512,768]{1,0:T(8,128)(2,1)} %param.29) | copy-start | bytes 2359300
  473.6 67.0 %copy-start.75 = (f32[768]{0:T(1024)S(1)}, f32[768]{0:T(1024)}, u32[]{:S(2)}) copy-start(f32[768]{0:T(1024)} %copy-done.74) | copy-start | bytes 9220
  476.4 189.7 %reduce-scatter.9.cloned.1.call-start = ((), (), s32[]{:S(2)}) async-start(), calls=%async_computation.9 | async-start | bytes 7864320 | tf_op jit(solution)/shard_map/reduce_scatter | solution.py:167
  556.6 109.6 %copy-start.49 = (f32[768]{0:T(1024)S(1)}, f32[768]{0:T(1024)}, u32[]{:S(2)}) copy-start(f32[768]{0:T(1024)} %convert_element_type.155) | copy-start | bytes 9220
  556.6 109.6 %copy-start.51 = (f32[512]{0:T(512)S(1)}, f32[512]{0:T(512)}, u32[]{:S(2)}) copy-start(f32[512]{0:T(512)} %copy-done.50) | copy-start | bytes 6148
  556.6 109.6 %copy-start.54 = (f32[512]{0:T(512)S(1)}, f32[512]{0:T(512)}, u32[]{:S(2)}) copy-start(f32[512]{0:T(512)} %copy-done.53) | copy-start | bytes 6148
  556.6 112.9 %copy-start.58 = (f32[512]{0:T(512)S(1)}, f32[512]{0:T(512)}, u32[]{:S(2)}) copy-start(f32[512]{0:T(512)} %copy-done.57) | copy-start | bytes 6148
  556.6 180.5 %all-gather.11.cloned.1.call-start = ((), (), s32[]{:S(2)}) async-start(), calls=%async_computation.10 | async-start | bytes 3932160 | tf_op jit(solution)/shard_map/all_gather | solution.py:174
  669.5 67.7 %copy-start.31 = (bf16[192,768]{1,0:T(8,128)(2,1)S(1)}, bf16[192,768]{1,0:T(8,128)(2,1)}, u32[]{:S(2)}) copy-start(bf16[192,768]{1,0:T(8,128)(2,1)} %param.19) | copy-start | bytes 884740
  670.2 70.1 %copy-start.59 = (f32[512]{0:T(512)}, f32[512]{0:T(512)S(1)}, u32[]{:S(2)}) copy-start(f32[512]{0:T(512)S(1)} %negate_multiply_fusion) | copy-start | bytes 6148
  673.0 248.5 %reduce-scatter.11.cloned.1.call-start = ((), (), s32[]{:S(2)}) async-start(), calls=%async_computation.11 | async-start | bytes 3932160 | tf_op jit(solution)/shard_map/reduce_scatter | solution.py:186
  742.9 12.0 %copy-start.7 = (f32[1,32,64,3,1,64]{5,2,3,1,4,0:T(8,128)S(1)}, f32[1,32,64,3,1,64]{5,2,3,1,4,0:T(8,128)}, u32[]{:S(2)}) copy-start(f32[1,32,64,3,1,64]{5,2,3,1,4,0:T(8,128)} %copy.191) | copy-start | bytes 4718596
  742.9 12.0 %copy-start.18 = (f32[1,32,64,3,64]{2,1,4,3,0:T(8,128)S(1)}, f32[1,32,64,3,64]{2,1,4,3,0:T(8,128)}, u32[]{:S(2)}) copy-start(f32[1,32,64,3,64]{2,1,4,3,0:T(8,128)} %reshape.798) | copy-start | bytes 4718596
  764.7 5.4 copy-start.33
  764.7 5.4 copy-start.38
  764.7 5.5 copy-start.3
  777.2 8.3 copy-start.63
  777.2 8.3 copy-start.66
  789.3 5.9 copy-start.5
  789.3 5.9 copy-start.28
  795.1 7.8 copy-start.13
  795.2 7.8 copy-start.22
  809.9 4.7 copy-start.20
  809.9 4.7 copy-start.25
  810.0 4.7 copy-start.52
  814.6 8.1 copy-start.9
  814.6 8.1 copy-start.10
  814.7 8.1 copy-start.45
  814.7 8.1 copy-start.47
  835.9 6.7 copy-start.87
  846.7 178.4 %all-reduce.8.cloned.1.call-start = ((), (), s32[]{:S(2)}) async-start(), calls=%async_computation.12 | async-start | bytes 14155776 | tf_op jit(solution)/shard_map/psum | solution.py:194
  847.0 7.1 copy-start.85
  847.0 7.1 copy-start.90
  854.1 4.2 copy-start.14
  863.7 43.8 %copy-start.76 = (f32[768]{0:T(1024)S(1)}, f32[768]{0:T(1024)}, u32[]{:S(2)}) copy-start(f32[768]{0:T(1024)} %get-tuple-element.40) | copy-start | bytes 9220
  863.7 57.8 %copy-start.16 = (f32[512,768]{1,0:T(8,128)S(1)}, f32[512,768]{1,0:T(8,128)}, u32[]{:S(2)}) copy-start(f32[512,768]{1,0:T(8,128)} %copy-done.15) | copy-start | bytes 4718596
  863.7 57.8 %copy-start.60 = (f32[512]{0:T(512)S(1)}, f32[512]{0:T(512)}, u32[]{:S(2)}) copy-start(f32[512]{0:T(512)} %copy-done.59) | copy-start | bytes 6148
  (36 other events, 73.9 us)
Sparse Core Ops, SparseCore 0:
  9.6 66.1 all-gather.4
  167.4 109.3 reduce-scatter.4
  280.3 64.0 all-gather.6
  359.0 109.3 reduce-scatter.6
  476.6 64.0 all-gather.8
  556.7 109.3 reduce-scatter.8
  673.1 64.0 all-gather.10
  846.8 59.8 reduce-scatter.10
  911.5 113.5 all-reduce.7
where the time goes:
time: 1050 us; the launch traced here: 1040 us
  waiting for transfers between devices  681 us (65%)
  matrix products  166 us (16%)
  local copies, waits for them, and re-layouts  73.7 us (7%)
  blocking collectives  57 us (5%)
  other arithmetic  45.5 us (4%)
  between operations  15.3 us (1%)
    reduce_scatter x1, waiting for transfers between devices, on_device(): lax.psum_scatter(rows_back(d_hidden, w_in), 'tensor', scatter_dimension=0...  109 us
    reduce_scatter x1, waiting for transfers between devices, on_device(): lax.psum_scatter(rows_product(attended, w_out), 'tensor', scatter_dimensi...  107 us
    reduce_scatter x1, waiting for transfers between devices, on_device(): lax.psum_scatter(rows_product(active, w_two), 'tensor', scatter_dimension...  107 us
    psum x1, waiting for transfers between devices, on_device(): lax.psum((d_w_qkv, d_b_qkv, d_w_out, d_w_in, d_b_in, d_w_two), 'dp')  101 us
    all_gather x1, waiting for transfers between devices, on_device(): second_full = lax.all_gather(d_second, 'tensor', axis=0, tiled=True)  64.1 us
    all_gather x1, waiting for transfers between devices, on_device(): middle_full = lax.all_gather(first_low, 'tensor', axis=0, tiled=True)  64.1 us
    all_gather x1, waiting for transfers between devices, on_device(): branch_full = lax.all_gather(d_branch, 'tensor', axis=0, tiled=True)  63.5 us
    all_gather x1, waiting for transfers between devices, on_device(): input_full = lax.all_gather(tokens, 'tensor', axis=0, tiled=True)  63.1 us
  transfers between devices with their start and end apart: 9, of which 8 were waited for; matrix products, arithmetic and copies ran while one was open for 3% of the time, Pallas kernels for 0%

commit v1 on v0

v1 whole, which is shorter than its diff:
```python
import functools
import math

import jax
import jax.numpy as jnp
from jax import lax
from jax.sharding import PartitionSpec as P

HEAD = 64
ROW_LEN = 2048
DOCS = 8
F32 = jnp.float32
BF16 = jnp.bfloat16


def dot(left, right, dims):
    return lax.dot_general(left, right, (dims, ((), ())), preferred_element_type=F32)


class Places:
    def __init__(self, dp, tensor):
        self.dp, self.tensor = dp, tensor
        self.row = lax.axis_index("dp")
        self.z = lax.axis_index("tensor")

    def bit(self, which):
        return (self.row >> which) & 1

    def swap(self, value, which):
        return lax.ppermute(value, "dp", [(d, d ^ (1 << which)) for d in range(self.dp)])

    def turn(self, value, step):
        size = self.tensor
        return lax.ppermute(value, "tensor", [(k, (k + step) % size) for k in range(size)])

    def onward(self, value, step):
        size = self.tensor
        pairs = [(k, k + step) for k in range(size) if 0 <= k + step < size]
        return lax.ppermute(value, "tensor", pairs)


def pair(own, other, bit):
    return jnp.where(bit == 0, jnp.stack([own, other]), jnp.stack([other, own]))


def gather_pieces(places, piece):
    parts = [piece] + [places.turn(piece, step) for step in range(1, places.tensor)]
    half = places.tensor // 2
    first, second = jnp.stack(parts[:half]), jnp.stack(parts[half:])
    first = pair(first, places.swap(first, 1), places.bit(1))
    second = pair(second, places.swap(second, 2), places.bit(2))
    first = pair(first, places.swap(first, 2), places.bit(2))
    second = pair(second, places.swap(second, 1), places.bit(1))
    first = pair(first, places.swap(first, 0), places.bit(0))
    second = pair(second, places.swap(second, 0), places.bit(0))
    second = jnp.swapaxes(second, 1, 2)
    return jnp.concatenate([first, second], axis=3)


def own_rows(places, weight):
    rows = weight.shape[0] // 8
    return lax.dynamic_slice_in_dim(weight, (places.row & 7) * rows, rows, 0)


def by_shard(pieces):
    ordered = jnp.transpose(pieces, (3, 1, 2, 0, 4, 5))
    return ordered.reshape(ordered.shape[0], -1, ordered.shape[-1])


def keep_and_send(value, bit, dim):
    kept = lax.dynamic_index_in_dim(value, bit, dim, keepdims=False)
    sent = lax.dynamic_index_in_dim(value, 1 - bit, dim, keepdims=False)
    return kept.astype(F32), sent.astype(BF16)


def reduce_pieces(places, grads, order):
    shards, rows, cols = grads.shape
    value = grads.reshape(shards, 2, 2, 2, rows // 8, cols)
    for which in (0,) + order:
        kept, sent = keep_and_send(value, places.bit(which), 1)
        value = kept + places.swap(sent, which).astype(F32)
    total = value[0]
    for step in range(1, shards):
        total = total + places.turn(value[step].astype(BF16), -step).astype(F32)
    for which in range(3, places.dp.bit_length() - 1):
        total = total + places.swap(total, which)
    low = total.astype(BF16)
    for which in order[::-1] + (0,):
        low = pair(low, places.swap(low, which), places.bit(which))
    return low.reshape(rows, cols).astype(F32)


def doc_tables(starts_row, places, count):
    spots = places.z * count + jnp.arange(count, dtype=jnp.int32)
    started = (spots[:, None] >= starts_row[None, :]).astype(jnp.int32)
    doc_ids = jnp.sum(started, axis=1) - 1
    onehot = (doc_ids[:, None] == jnp.arange(DOCS, dtype=jnp.int32)[None, :]).astype(jnp.int32)
    finish = jnp.concatenate([starts_row[1:], jnp.full((1,), ROW_LEN, jnp.int32)])
    own_start = jnp.sum(onehot * starts_row[None, :], axis=1)
    own_len = jnp.sum(onehot * (finish - starts_row)[None, :], axis=1)
    angles = 0.5 * math.pi * (spots - own_start).astype(F32) / own_len.astype(F32)
    return angles, doc_ids


def doc_at(starts_row, spot):
    return jnp.sum((spot >= starts_row).astype(jnp.int32)) - 1


def shift_shards(state, step):
    return jnp.roll(state, step, axis=0)


def norm_parts(rows_in):
    centred = rows_in - jnp.mean(rows_in, axis=-1, keepdims=True)
    spread = jnp.mean(centred * centred, axis=-1, keepdims=True)
    scale = lax.rsqrt(spread + 1e-05)
    return centred * scale, scale


def norm_back(grad, normed, scale, gain):
    e = grad * gain
    d_rows = scale * (
        e
        - jnp.mean(e, axis=-1, keepdims=True)
        - normed * jnp.mean(e * normed, axis=-1, keepdims=True)
    )
    return d_rows, jnp.sum(grad * normed, axis=0), jnp.sum(grad, axis=0)


def gelu_parts(v):
    k = math.sqrt(2 / math.pi)
    t = jnp.tanh(k * (v + 0.044715 * v * v * v))
    slope = 0.5 * (1 + t) + 0.5 * v * (1 - t * t) * k * (1 + 3 * 0.044715 * v * v)
    return 0.5 * v * (1 + t), slope


def on_device(dp, tensor, tokens, starts, w_qkv, b_qkv, w_out, b_out, gain_one, shift_one, w_in, b_in,
              w_two, b_two, gain_two, shift_two, cotangent):
    places = Places(dp, tensor)
    count = tokens.shape[0]
    width = tokens.shape[1]
    heads = w_qkv.shape[1] // (3 * HEAD)
    f = lambda a: a.astype(F32)
    qkv_all = by_shard(gather_pieces(places, own_rows(places, w_qkv)))
    rest = jnp.concatenate([own_rows(places, w_out), own_rows(places, w_in), own_rows(places, w_two)])
    rest_all = gather_pieces(places, rest)
    n_out, n_in = w_out.shape[0] // 8, w_in.shape[0] // 8
    out_all = by_shard(rest_all[..., :n_out, :])
    in_all = by_shard(rest_all[..., n_out:n_out + n_in, :])
    two_all = by_shard(rest_all[..., n_out + n_in:, :])
    biases = jnp.concatenate([b_qkv, b_in]).reshape(1, -1)
    bias_all = jnp.concatenate([biases] + [places.turn(biases, s) for s in range(1, tensor)])
    bias_qkv, bias_in = f(bias_all[:, :b_qkv.shape[0]]), f(bias_all[:, b_qkv.shape[0]:])

    row = starts[0]
    angles, docs = doc_tables(row, places, count)
    base = places.z * count
    first_doc, last_doc = doc_at(row, base), doc_at(row, base + count - 1)
    opening = (docs == first_doc).astype(F32)
    tail = (docs == last_doc).astype(F32)
    spot = jnp.arange(count)
    mask = jnp.where((docs[:, None] == docs[None, :]) & (spot[:, None] >= spot[None, :]),
                     jnp.cos(angles[:, None] - angles[None, :]), 0.0)
    cosine, sines = jnp.cos(angles)[:, None], jnp.sin(angles)[:, None]

    mixed = jnp.einsum("td,jdc->jtc", tokens, qkv_all, preferred_element_type=F32) + bias_qkv[:, None]
    parts = mixed.reshape(tensor, count, heads, 3, HEAD)
    query, key, value = (jnp.transpose(parts[:, :, :, i], (0, 2, 1, 3)) for i in range(3))
    query, key, value = jax.nn.relu(query).astype(BF16), jax.nn.relu(key).astype(BF16), value.astype(BF16)
    ones = jnp.ones(value.shape[:-1] + (1,), BF16)
    value_one = jnp.concatenate([value, ones], axis=-1)

    def feats(a, weight):
        return jnp.concatenate([f(a) * (cosine * weight), f(a) * (sines * weight)], axis=-1).astype(BF16)

    fq_open = feats(query, opening[:, None])
    fk_tail = feats(key, tail[:, None])
    state = jnp.einsum("jhtf,jhtv->jhfv", fk_tail, value_one, preferred_element_type=F32).astype(BF16)
    carried = jnp.zeros(state.shape, F32)
    for step in range(1, tensor):
        link = (doc_at(row, base - (step - 1) * count - 1) == first_doc).astype(F32)
        carried = carried + link * f(shift_shards(places.onward(state, step), step))
    carried = carried.astype(BF16)
    scores = jnp.einsum("jhtf,jhsf->jhts", query, key, preferred_element_type=F32) * mask
    scores = scores.astype(BF16)
    sums = jnp.einsum("jhts,jhsv->jhtv", scores, value_one, preferred_element_type=F32) + jnp.einsum(
        "jhtf,jhfv->jhtv", fq_open, carried, preferred_element_type=F32)
    den_raw = sums[..., HEAD:]
    den = jnp.maximum(den_raw, 1.0)
    o = sums[..., :HEAD] / den
    attended = jnp.transpose(o, (2, 0, 1, 3)).reshape(count, width).astype(BF16)
    w_out_full = out_all.reshape(width, width)
    r1 = f(tokens) + dot(attended, w_out_full, ((1,), (0,))) + f(b_out)
    n1, s1 = norm_parts(r1)
    first = (n1 * f(gain_one) + f(shift_one)).astype(BF16)
    hidden = jnp.einsum("td,jdc->jtc", first, in_all, preferred_element_type=F32) + bias_in[:, None]
    act, slope = gelu_parts(hidden)
    act = act.astype(BF16)
    second = jnp.einsum("jtc,jcd->td", act, two_all, preferred_element_type=F32) + f(b_two)
    n2, s2 = norm_parts(f(first) + second)
    block_out = (n2 * f(gain_two) + f(shift_two)).astype(BF16)

    d_r2, d_gain_two, d_shift_two = norm_back(f(cotangent), n2, s2, f(gain_two))
    d_second = d_r2.astype(BF16)
    d_b_two = jnp.sum(f(d_second), axis=0)
    g_two = jnp.einsum("td,jtc->jdc", d_second, act, preferred_element_type=F32)
    d_w_two = reduce_pieces(places, g_two, (1, 2)).T
    d_hidden = (jnp.einsum("td,jcd->jtc", d_second, two_all, preferred_element_type=F32) * slope).astype(BF16)
    d_b_in = jnp.sum(f(d_hidden), axis=1)
    g_in = jnp.einsum("td,jtc->jdc", first, d_hidden, preferred_element_type=F32)
    d_w_in = reduce_pieces(places, g_in, (2, 1))
    d_first = jnp.einsum("jtc,jdc->td", d_hidden, in_all, preferred_element_type=F32) + d_r2
    d_r1, d_gain_one, d_shift_one = norm_back(d_first, n1, s1, f(gain_one))
    d_branch = d_r1.astype(BF16)
    d_b_out = jnp.sum(f(d_branch), axis=0)
    g_out = dot(attended, d_branch, ((0,), (0,))).reshape(tensor, -1, width)
    d_w_out = reduce_pieces(places, g_out, (1, 2))
    g = dot(d_branch, w_out_full, ((1,), (1,))).reshape(count, tensor, heads, HEAD)
    g = jnp.transpose(g, (1, 2, 0, 3))
    d_num = g / den
    d_den = jnp.where(den_raw > 1.0, -jnp.sum(g * o, axis=-1, keepdims=True) / den, 0.0)
    d_sums = jnp.concatenate([d_num, d_den], axis=-1).astype(BF16)
    d_carried = jnp.einsum("jhtf,jhtv->jhfv", fq_open, d_sums, preferred_element_type=F32).astype(BF16)
    d_state = jnp.zeros(state.shape, F32)
    for step in range(1, tensor):
        link = (doc_at(row, base + step * count) == last_doc).astype(F32)
        d_state = d_state + link * f(shift_shards(places.onward(d_carried, -step), -step))
    d_state = d_state.astype(BF16)
    d_scores = (jnp.einsum("jhtv,jhsv->jhts", d_sums, value_one, preferred_element_type=F32) * mask).astype(BF16)
    d_fq = jnp.einsum("jhtv,jhfv->jhtf", d_sums, carried, preferred_element_type=F32) * opening[:, None]
    d_query = jnp.einsum("jhts,jhsf->jhtf", d_scores, key, preferred_element_type=F32) + (
        d_fq[..., :HEAD] * cosine + d_fq[..., HEAD:] * sines)
    d_fk = jnp.einsum("jhtv,jhfv->jhtf", value_one, d_state, preferred_element_type=F32) * tail[:, None]
    d_key = jnp.einsum("jhts,jhtf->jhsf", d_scores, query, preferred_element_type=F32) + (
        d_fk[..., :HEAD] * cosine + d_fk[..., HEAD:] * sines)
    d_value = jnp.einsum("jhts,jhtv->jhsv", scores, d_sums[..., :HEAD], preferred_element_type=F32) + jnp.einsum(
        "jhtf,jhfv->jhtv", fk_tail, d_state[..., :HEAD], preferred_element_type=F32)
    d_query = jnp.where(query > 0, d_query, 0.0)
    d_key = jnp.where(key > 0, d_key, 0.0)
    d_mixed = jnp.stack([d_query, d_key, d_value], axis=3).astype(BF16)
    d_mixed = jnp.transpose(d_mixed, (0, 2, 1, 3, 4)).reshape(tensor, count, -1)
    d_b_qkv = jnp.sum(f(d_mixed), axis=1)
    g_qkv = jnp.einsum("td,jtc->jdc", tokens, d_mixed, preferred_element_type=F32)
    d_w_qkv = reduce_pieces(places, g_qkv, (2, 1))
    d_tokens = (jnp.einsum("jtc,jdc->td", d_mixed, qkv_all, preferred_element_type=F32) + d_r1).astype(BF16)

    shared = jnp.concatenate([d_b_out, d_gain_one, d_shift_one, d_b_two, d_gain_two, d_shift_two])
    split = jnp.concatenate([d_b_qkv, d_b_in], axis=1)
    turned = jnp.concatenate([split[::-1], split[::-1]])
    split = lax.dynamic_slice_in_dim(turned, tensor - 1 - places.z, tensor, 0)
    summed = lax.psum(jnp.concatenate([shared, split.reshape(-1)]), ("dp", "tensor"))
    d_b_out, d_gain_one, d_shift_one, d_b_two, d_gain_two, d_shift_two = jnp.split(summed[:6 * width], 6)
    split = lax.dynamic_index_in_dim(summed[6 * width:].reshape(tensor, -1), places.z, 0, keepdims=False)
    d_b_qkv, d_b_in = split[:b_qkv.shape[0]], split[b_qkv.shape[0]:]
    return (block_out, d_tokens, d_w_qkv, d_b_qkv, d_w_out, d_b_out, d_gain_one, d_shift_one, d_w_in, d_b_in,
            d_w_two, d_b_two, d_gain_two, d_shift_two)


def solution(mesh):
    sizes = dict(mesh.shape)
    rows = P(("dp", "tensor"), None)
    wide, tall, cut, whole = P(None, "tensor"), P("tensor", None), P("tensor"), P()
    in_specs = (rows, P("dp", None), wide, cut, tall, whole, whole, whole, wide, cut, tall, whole, whole, whole, rows)
    out_specs = (rows, rows, wide, cut, tall, whole, whole, whole, wide, cut, tall, whole, whole, whole)
    return jax.shard_map(
        functools.partial(on_device, sizes["dp"], sizes["tensor"]),
        mesh=mesh, in_specs=in_specs, out_specs=out_specs, check_vma=False,
    )
```

time: 1050 us -> 421 us (0.40)
  waiting for transfers between devices: 681 us -> 134 us
  matrix products: 166 us -> 68.2 us
  starting transfers between devices: 0.62 us -> 82.9 us
  local copies, waits for them, and re-layouts: 73.7 us -> 39.2 us
  blocking collectives: 57 us -> 40.1 us
    reduce_scatter x4 -> x0, waiting for transfers between devices: 324 us -> none  [the longest x1 109 us: on_device(): lax.psum_scatter(rows_back(d_hidden, w_in), 'tensor', scatter_dimension=0...]
    all_gather x4 -> x0, waiting for transfers between devices: 255 us -> none  [the longest x1 64.1 us: on_device(): second_full = lax.all_gather(d_second, 'tensor', axis=0, tiled=True)]
    ppermute x0 -> x63, waiting for transfers between devices: none -> 134 us  [the longest x36 102 us: swap(): lax.ppermute(value, 'dp', [(d, d ^ 1 << which) for d in range(self.dp)])]
    psum x1 -> x0, waiting for transfers between devices: 101 us -> none  [on_device(): lax.psum((d_w_qkv, d_b_qkv, d_w_out, d_w_in, d_b_in, d_w_two), 'dp')]
    dot_general x31 -> x24, matrix products: 166 us -> 68.2 us  [the longest x1 9.17 us: on_device(): jnp.einsum('td,jcd->jtc', d_second, two_all, preferred_element_type=F32)]
    ppermute x0 -> x63, starting transfers between devices: none -> 82.9 us  [the longest x21 39.5 us: turn(): lax.ppermute(value, 'tensor', [(k, (k + step) % size) for k in range(size)])]
    unnamed x189 -> x68, local copies, waits for them, and re-layouts: 29.2 us -> 8.69 us
    reduce_sum x12 -> x7, other arithmetic: 22.6 us -> 4.63 us  [the longest x1 1.56 us: on_device(): d_b_two = jnp.sum(f(d_second), axis=0)]
  transfers between devices with their start and end apart: 9 -> 63, of which waited for: 8 -> 27; matrix products, arithmetic and copies ran while one was open for 3% -> 26% of each run, Pallas kernels for 0% -> 0%
where the time goes in v1:
time: 421 us; the launch traced here: 416 us
  waiting for transfers between devices  134 us (32%)
  starting transfers between devices  82.9 us (20%)
  matrix products  68.2 us (16%)
  other arithmetic  44.1 us (10%)
  blocking collectives  40.1 us (10%)
  local copies, waits for them, and re-layouts  39.2 us (9%)
  between operations  7.77 us (2%)
    ppermute x36, waiting for transfers between devices, swap(): lax.ppermute(value, 'dp', [(d, d ^ 1 << which) for d in range(self.dp)])  102 us
    psum x1, blocking collectives, on_device(): lax.psum(jnp.concatenate([shared, split.reshape(-1)]), ('dp', 'tensor'))  40.1 us
    ppermute x21, starting transfers between devices, turn(): lax.ppermute(value, 'tensor', [(k, (k + step) % size) for k in range(size)])  39.5 us
    ppermute x21, waiting for transfers between devices, turn(): lax.ppermute(value, 'tensor', [(k, (k + step) % size) for k in range(size)])  31.9 us
    ppermute x36, starting transfers between devices, swap(): lax.ppermute(value, 'dp', [(d, d ^ 1 << which) for d in range(self.dp)])  31.6 us
    ppermute x6, starting transfers between devices, onward(): return lax.ppermute(value, 'tensor', pairs)  11.8 us
    convert_element_type x12, local copies, waits for them, and re-layouts, keep_and_send(): return (kept.astype(F32), sent.astype(BF16))  11 us
    add x8, other arithmetic, reduce_pieces(): value = kept + places.swap(sent, which).astype(F32)  9.48 us
  transfers between devices with their start and end apart: 63, of which 27 were waited for; matrix products, arithmetic and copies ran while one was open for 26% of the time, Pallas kernels for 0%

profile of v1, /device:TPU:0, one launch (start us, length us, event | category | flops | bytes accessed | tf_op | source)
XLA Modules:
  0.0 416.2 jit_solution(15520140502404136864)
XLA Ops:
  2.6 5.1 %collective-permute-start.20 = (bf16[216,768]{1,0:T(8,128)(2,1)S(1)}, bf16[216,768]{1,0:T(8,128)(2,1)S(1)}, u32[]{:S(2)}, u32[]{:S(2)}) collective-permute-start(bf16[216,768]{1,0:T(8,128)(2,1)S(1)} %get-tuple-element.142), channel_id=1, source_target_pairs={{0,3},{1,0},{2,1},{3,2},{4,7},{5,4},{6,5},{7,6},{8,11},{9,8},{10,9... | collective-permute-start | bytes 995336 | tf_op jit(solution)/shard_map/ppermute | solution.py:34
  9.0 2.6 collective-permute-start.10
  11.6 1.9 collective-permute-start.9
  16.5 2.3 cosine_select_fusion
  26.0 9.4 %collective-permute-start.15 = (bf16[216,768]{1,0:T(8,128)(2,1)S(1)}, bf16[216,768]{1,0:T(8,128)(2,1)S(1)}, u32[]{:S(2)}, u32[]{:S(2)}) collective-permute-start(bf16[216,768]{1,0:T(8,128)(2,1)S(1)} %get-tuple-element.142), channel_id=1, source_target_pairs={{0,1},{1,2},{2,3},{3,0},{4,5},{5,6},{6,7},{7,4},{8,9},{9,10},{10,1... | collective-permute-start | bytes 995336 | tf_op jit(solution)/shard_map/ppermute | solution.py:34
  37.0 5.2 %collective-permute-done.5 = bf16[96,576]{1,0:T(8,128)(2,1)S(1)} collective-permute-done((bf16[96,576]{1,0:T(8,128)(2,1)S(1)}, bf16[96,576]{1,0:T(8,128)(2,1)S(1)}, u32[]{:S(2)}, u32[]{:S(2)}) %collective-permute-start.5) | collective-permute-done | bytes 110624 | tf_op jit(solution)/shard_map/ppermute | solution.py:34
  42.4 3.4 collective-permute-done.4
  47.4 2.1 collective-permute-done
  56.5 2.1 collective-permute-done.1
  60.8 18.3 %collective-permute-done.7 = bf16[2,2,96,576]{3,2,1,0:T(8,128)(2,1)S(1)} collective-permute-done((bf16[2,2,96,576]{3,2,1,0:T(8,128)(2,1)S(1)}, bf16[2,2,96,576]{3,2,1,0:T(8,128)(2,1)S(1)}, u32[]{:S(2)}, u32[]{:S(2)}) %collective-permute-start.7) | collective-permute-done | bytes 442400 | tf_op jit(solution)/shard_map/ppermute | solution.py:30
  87.0 2.5 broadcast_add_fusion
  91.2 2.7 collective-permute-start.12
  93.9 3.7 collective-permute-start.13
  99.2 1.9 multiply_convert_fusion.1
  101.1 2.0 fusion.66
  103.1 9.1 %collective-permute-done.22 = bf16[2,2,216,768]{3,2,0,1:T(8,128)(2,1)S(1)} collective-permute-done((bf16[2,2,216,768]{3,2,0,1:T(8,128)(2,1)S(1)}, bf16[2,2,216,768]{3,2,0,1:T(8,128)(2,1)S(1)}, u32[]{:S(2)}, u32[]{:S(2)}) %collective-permute-start.22) | collective-permute-done | bytes 1327136 | tf_op jit(solution)/shard_map/ppermute | solution.py:30
  112.2 2.1 maximum_select_fusion.4
  114.5 1.7 maximum_select_fusion.3
  119.6 3.5 fusion.7
  123.2 3.0 pad_maximum_fusion.1
  127.7 4.8 %fusion.56 = f32[4,768,512]{1,2,0:T(8,128)} fusion(bf16[4,768,768]{2,1,0:T(8,128)(2,1)S(1)} %bitcast.427, f32[512,768]{1,0:T(8,128)S(1)} %get-tuple-element.171, f32[768]{0:T(1024)S(1)} %convert_element_type.549, f32[768]{0:T(1024)S(1)} %convert_element_type.548, f32[512]{0:T(512)S(1)} %add_rsqrt_fusion.1, f32[512]{0:T(512)S(1)} %broadcast_multiply_fusion.5), kind=kOutput, calls=%fused_computation.163 | convolution fusion | flops 2417885184 | bytes 12593152 | tf_op jit(solution)/shard_map/td,jdc->jtc/dot_general | solution.py:196
  132.5 6.3 %fusion.145 = (f32[512]{0:T(512)S(1)}, f32[512,768]{1,0:T(8,128)S(1)}) fusion(f32[768]{0:T(1024)S(1)} %convert_element_type.554, bf16[4,768,768]{2,1,0:T(8,128)(2,1)S(1)} %bitcast.431, f32[4,768,512]{1,2,0:T(8,128)} %fusion.56, f32[4,768]{1,0:T(4,128)S(1)} %fusion.96, f32[768]{0:T(1024)S(1)} %convert_element_type.549, f32[768]{0:T(1024)S(1)} %convert_element_type.548, ...), kind=kOutput, calls=%fused_computation.357 | convolution fusion | flops 2435186176 | bytes 14183424 | tf_op jit(solution)/shard_map/jtc,jcd->td/dot_general | solution.py:199
  142.3 9.2 %convert_reduce_fusion = (f32[4,768]{1,0:T(4,128)S(1)}, bf16[4,512,768]{2,1,0:T(8,128)(2,1)}) fusion(f32[4,768,512]{1,2,0:T(8,128)} %fusion.56, f32[4,768]{1,0:T(4,128)S(1)} %fusion.96, bf16[4,768,768]{2,1,0:T(8,128)(2,1)S(1)} %bitcast.432, f32[512,768]{1,0:T(8,128)S(1)} %get-tuple-element.97), kind=kOutput, calls=%fused_computation.12 | convolution fusion | flops 2450912256 | bytes 15753216 | tf_op jit(solution)/shard_map/td,jcd->jtc/dot_general | solution.py:208
  151.5 5.0 %multiply_reduce_fusion = (f32[768]{0:T(1024)S(1)}, f32[512]{0:T(512)S(1)}, f32[512]{0:T(512)S(1)}, f32[768]{0:T(1024)S(1)}, f32[512,768]{1,0:T(8,128)S(1)}) fusion(f32[512,768]{1,0:T(8,128)S(1)} %get-tuple-element.171, f32[512]{0:T(512)S(1)} %add_rsqrt_fusion.1, f32[512]{0:T(512)S(1)} %broadcast_multiply_fusion.5, f32[768]{0:T(1024)S(1)} %convert_element_type.548, ...), kind=kOutput, calls=%fused_computation.99 | convolution fusion | flops 2419848704 | bytes 12600320 | tf_op jit(solution)/shard_map/jtc,jdc->td/dot_general | solution.py:212
  164.8 1.9 multiply_convert_fusion
  166.7 5.3 %fusion.54 = f32[4,768,768]{1,2,0:T(8,128)} fusion(bf16[4,512,768]{2,1,0:T(8,128)(2,1)S(1)} %copy-done.23, f32[512,768]{1,0:T(8,128)S(1)} %get-tuple-element.171, f32[768]{0:T(1024)S(1)} %convert_element_type.549, f32[768]{0:T(1024)S(1)} %convert_element_type.548, f32[512]{0:T(512)S(1)} %add_rsqrt_fusion.1, f32[512]{0:T(512)S(1)} %broadcast_multiply_fusion.5), kind=kOutput, calls=%fused_computation.161 | convolution fusion | flops 2417885184 | bytes 14166016 | tf_op jit(solution)/shard_map/td,jtc->jdc/dot_general | solution.py:210
  172.0 5.2 %fusion.51 = f32[4,768,768]{1,2,0:T(8,128)S(1)} fusion(f32[512,768]{1,0:T(8,128)S(1)} %get-tuple-element.97, f32[4,768,512]{1,2,0:T(8,128)} %fusion.56, f32[4,768]{1,0:T(4,128)S(1)} %fusion.96), kind=kOutput, calls=%fused_computation.158 | convolution fusion | flops 2432040960 | bytes 17313792 | tf_op jit(solution)/shard_map/td,jtc->jdc/dot_general | solution.py:206
  177.2 2.7 convolution_multiply_fusion.1
  180.8 1.9 copy-done.2
  183.7 4.2 %fusion.8 = bf16[4,2,2,96,768]{4,3,0,2,1:T(8,128)(2,1)} fusion(f32[4,2,2,2,96,768]{5,4,3,2,1,0:T(8,128)} %bitcast.421, s32[]{:T(128)S(6)} %select_n.542), kind=kLoop, calls=%fused_computation.37 | loop fusion | bytes 4718596 | tf_op jit(solution)/shard_map/convert_element_type | solution.py:73
  188.3 2.0 fusion.38
  190.4 1.7 fusion.9
  200.8 4.9 %convolution_bitcast_fusion = f32[4,768,576]{1,2,0:T(8,128)} fusion(bf16[4,512,576]{1,2,0:T(8,128)(2,1)S(1)} %bitcast.412, bf16[512,768]{1,0:T(8,128)(2,1)S(1)} %copy-done.16), kind=kOutput, calls=%fused_computation.27 | convolution fusion | flops 1811939328 | bytes 10223616 | tf_op jit(solution)/shard_map/td,jtc->jdc/dot_general | solution.py:243
  205.7 8.5 %copy.194 = f32[4,768,576]{2,1,0:T(8,128)} copy(f32[4,768,576]{1,2,0:T(8,128)} %convolution_bitcast_fusion) | data formatting | bytes 14155776 | tf_op jit(solution)/shard_map/td,jtc->jdc/transpose | solution.py:243
  214.2 5.9 %fusion.33 = bf16[512,768]{1,0:T(8,128)(2,1)} fusion(f32[512,768]{1,0:T(8,128)} %copy-done.4, bf16[4,512,576]{1,2,0:T(8,128)(2,1)S(1)} %bitcast.413, bf16[4,768,576]{2,1,0:T(8,128)(2,1)} %bitcast.434), kind=kOutput, calls=%fused_computation.90 | convolution fusion | flops 1812725760 | bytes 8257536 | tf_op jit(solution)/shard_map/jtc,jdc->td/dot_general | solution.py:245
  222.9 3.6 fusion.13
  227.0 3.5 collective-permute-done.37
  231.5 4.3 %collective-permute-done.38 = bf16[4,24,768]{2,1,0:T(8,128)(2,1)S(1)} collective-permute-done((bf16[4,24,768]{2,1,0:T(8,128)(2,1)S(1)}, bf16[4,24,768]{2,1,0:T(8,128)(2,1)S(1)}, u32[]{:S(2)}, u32[]{:S(2)}) %collective-permute-start.38) | collective-permute-done | bytes 147488 | tf_op jit(solution)/shard_map/ppermute | solution.py:30
  235.8 2.6 collective-permute-start.41
  238.4 4.8 %collective-permute-start.40 = (bf16[24,768]{1,0:T(8,128)(2,1)S(1)}, bf16[24,768]{1,0:T(8,128)(2,1)S(1)}, u32[]{:S(2)}, u32[]{:S(2)}) collective-permute-start(bf16[24,768]{1,0:T(8,128)(2,1)S(1)} %get-tuple-element.155), channel_id=1, source_target_pairs={{0,2},{1,3},{2,0},{3,1},{4,6},{5,7},{6,4},{7,5},{8,10},{9,11},{10,... | collective-permute-start | bytes 110600 | tf_op jit(solution)/shard_map/ppermute | solution.py:34
  243.3 40.1 %psum.7 = f32[9984]{0:T(1024)S(1)} all-reduce(f32[9984]{0:T(1024)S(1)} %constant_dynamic-update-slice_fusion), channel_id=1, replica_groups=mesh['dp'=8,'tensor'=4] {'dp','tensor'}, use_global_device_ids=true, to_apply=%region_28.29 | all-reduce | flops 9984 | bytes 79872 | tf_op jit(solution)/shard_map/psum | solution.py:251
  283.5 2.3 collective-permute-start.42
  288.0 1.8 collective-permute-start.43
  289.8 3.1 bitcast_add_fusion.2
  296.3 3.7 bitcast_add_fusion.1
  300.0 16.4 %collective-permute-done.28 = bf16[4,2,96,576]{3,2,1,0:T(8,128)(2,1)S(1)} collective-permute-done((bf16[4,2,96,576]{3,2,1,0:T(8,128)(2,1)S(1)}, bf16[4,2,96,576]{3,2,1,0:T(8,128)(2,1)S(1)}, u32[]{:S(2)}, u32[]{:S(2)}) %collective-permute-start.28) | collective-permute-done | bytes 884768 | tf_op jit(solution)/shard_map/ppermute | solution.py:30
  319.3 9.2 %collective-permute-done.29 = bf16[4,96,576]{2,1,0:T(8,128)(2,1)S(1)} collective-permute-done((bf16[4,96,576]{2,1,0:T(8,128)(2,1)S(1)}, bf16[4,96,576]{2,1,0:T(8,128)(2,1)S(1)}, u32[]{:S(2)}, u32[]{:S(2)}) %collective-permute-start.29) | collective-permute-done | bytes 442400 | tf_op jit(solution)/shard_map/ppermute | solution.py:30
  328.7 2.1 collective-permute-start.31
  333.5 2.7 collective-permute-done.32
  336.2 2.6 collective-permute-done.31
  341.0 19.8 %collective-permute-done.33 = bf16[96,576]{1,0:T(8,128)(2,1)S(1)} collective-permute-done((bf16[96,576]{1,0:T(8,128)(2,1)S(1)}, bf16[96,576]{1,0:T(8,128)(2,1)S(1)}, u32[]{:S(2)}, u32[]{:S(2)}) %collective-permute-start.33) | collective-permute-done | bytes 110624 | tf_op jit(solution)/shard_map/ppermute | solution.py:30
  362.6 2.1 collective-permute-start.56
  364.7 5.1 %collective-permute-done.34 = bf16[2,96,576]{2,1,0:T(8,128)(2,1)S(1)} collective-permute-done((bf16[2,96,576]{2,1,0:T(8,128)(2,1)S(1)}, bf16[2,96,576]{2,1,0:T(8,128)(2,1)S(1)}, u32[]{:S(2)}, u32[]{:S(2)}) %collective-permute-start.34) | collective-permute-done | bytes 221216 | tf_op jit(solution)/shard_map/ppermute | solution.py:30
  370.1 2.8 collective-permute-done.47
  375.0 2.8 collective-permute-start.48
  379.6 2.2 collective-permute-done.50
  382.8 5.3 %collective-permute-done.49 = bf16[96,768]{1,0:T(8,128)(2,1)S(1)} collective-permute-done((bf16[96,768]{1,0:T(8,128)(2,1)S(1)}, bf16[96,768]{1,0:T(8,128)(2,1)S(1)}, u32[]{:S(2)}, u32[]{:S(2)}) %collective-permute-start.49) | collective-permute-done | bytes 147488 | tf_op jit(solution)/shard_map/ppermute | solution.py:34
  389.1 2.0 collective-permute-done.59
  391.1 6.5 %collective-permute-done.58 = bf16[96,768]{1,0:T(8,128)(2,1)S(1)} collective-permute-done((bf16[96,768]{1,0:T(8,128)(2,1)S(1)}, bf16[96,768]{1,0:T(8,128)(2,1)S(1)}, u32[]{:S(2)}, u32[]{:S(2)}) %collective-permute-start.58) | collective-permute-done | bytes 147488 | tf_op jit(solution)/shard_map/ppermute | solution.py:34
  398.7 2.0 copy.202
  402.0 2.4 collective-permute-done.60
  405.5 3.6 collective-permute-done.52
  409.3 1.9 collective-permute-done.61
  414.0 2.0 copy.203
  (327 shorter events, 91.0 us)
Async XLA Ops:
  2.6 48.5 %collective-permute-start.20 = (bf16[216,768]{1,0:T(8,128)(2,1)S(1)}, bf16[216,768]{1,0:T(8,128)(2,1)S(1)}, u32[]{:S(2)}, u32[]{:S(2)}) collective-permute-start(bf16[216,768]{1,0:T(8,128)(2,1)S(1)} %get-tuple-element.142), channel_id=1, source_target_pairs={{0,3},{1,0},{2,1},{3,2},{4,7},{5,4},{6,5},{7,6},{8,11},{9,8},{10,9... | collective-permute-start | bytes 995336 | tf_op jit(solution)/shard_map/ppermute | solution.py:34
  7.7 43.4 %collective-permute-start.19 = (bf16[216,768]{1,0:T(8,128)(2,1)S(1)}, bf16[216,768]{1,0:T(8,128)(2,1)S(1)}, u32[]{:S(2)}, u32[]{:S(2)}) collective-permute-start(bf16[216,768]{1,0:T(8,128)(2,1)S(1)} %get-tuple-element.142), channel_id=1, source_target_pairs={{0,2},{1,3},{2,0},{3,1},{4,6},{5,7},{6,4},{7,5},{8,10},{9,11},{10,... | collective-permute-start | bytes 995336 | tf_op jit(solution)/shard_map/ppermute | solution.py:34
  8.5 17.5 %collective-permute-start.11 = (bf16[1,1344]{1,0:T(2,128)(2,1)S(1)}, bf16[1,1344]{1,0:T(2,128)(2,1)S(1)}, u32[]{:S(2)}, u32[]{:S(2)}) collective-permute-start(bf16[1,1344]{1,0:T(2,128)(2,1)S(1)} %reshape.1789), channel_id=1, source_target_pairs={{0,3},{1,0},{2,1},{3,2},{4,7},{5,4},{6,5},{7,6},{8,11},{9,8},{10,9... | collective-permute-start | bytes 8072 | tf_op jit(solution)/shard_map/ppermute | solution.py:34
  9.0 26.4 %collective-permute-start.10 = (bf16[1,1344]{1,0:T(2,128)(2,1)S(1)}, bf16[1,1344]{1,0:T(2,128)(2,1)S(1)}, u32[]{:S(2)}, u32[]{:S(2)}) collective-permute-start(bf16[1,1344]{1,0:T(2,128)(2,1)S(1)} %reshape.1789), channel_id=1, source_target_pairs={{0,2},{1,3},{2,0},{3,1},{4,6},{5,7},{6,4},{7,5},{8,10},{9,11},{10,... | collective-permute-start | bytes 8072 | tf_op jit(solution)/shard_map/ppermute | solution.py:34
  11.6 23.9 %collective-permute-start.9 = (bf16[1,1344]{1,0:T(2,128)(2,1)S(1)}, bf16[1,1344]{1,0:T(2,128)(2,1)S(1)}, u32[]{:S(2)}, u32[]{:S(2)}) collective-permute-start(bf16[1,1344]{1,0:T(2,128)(2,1)S(1)} %reshape.1789), channel_id=1, source_target_pairs={{0,1},{1,2},{2,3},{3,0},{4,5},{5,6},{6,7},{7,4},{8,9},{9,10},{10,1... | collective-permute-start | bytes 8072 | tf_op jit(solution)/shard_map/ppermute | solution.py:34
  26.0 26.9 %collective-permute-start.15 = (bf16[216,768]{1,0:T(8,128)(2,1)S(1)}, bf16[216,768]{1,0:T(8,128)(2,1)S(1)}, u32[]{:S(2)}, u32[]{:S(2)}) collective-permute-start(bf16[216,768]{1,0:T(8,128)(2,1)S(1)} %get-tuple-element.142), channel_id=1, source_target_pairs={{0,1},{1,2},{2,3},{3,0},{4,5},{5,6},{6,7},{7,4},{8,9},{9,10},{10,1... | collective-permute-start | bytes 995336 | tf_op jit(solution)/shard_map/ppermute | solution.py:34
  35.4 6.8 %collective-permute-start.5 = (bf16[96,576]{1,0:T(8,128)(2,1)S(1)}, bf16[96,576]{1,0:T(8,128)(2,1)S(1)}, u32[]{:S(2)}, u32[]{:S(2)}) collective-permute-start(bf16[96,576]{1,0:T(8,128)(2,1)S(1)} %copy.217), channel_id=1, source_target_pairs={{0,3},{1,0},{2,1},{3,2},{4,7},{5,4},{6,5},{7,6},{8,11},{9,8},{10,9... | collective-permute-start | bytes 331784 | tf_op jit(solution)/shard_map/ppermute | solution.py:34
  35.4 10.3 %collective-permute-start.4 = (bf16[96,576]{1,0:T(8,128)(2,1)S(1)}, bf16[96,576]{1,0:T(8,128)(2,1)S(1)}, u32[]{:S(2)}, u32[]{:S(2)}) collective-permute-start(bf16[96,576]{1,0:T(8,128)(2,1)S(1)} %copy.217), channel_id=1, source_target_pairs={{0,2},{1,3},{2,0},{3,1},{4,6},{5,7},{6,4},{7,5},{8,10},{9,11},{10,... | collective-permute-start | bytes 331784 | tf_op jit(solution)/shard_map/ppermute | solution.py:34
  42.2 7.3 %collective-permute-start = (bf16[96,576]{1,0:T(8,128)(2,1)S(1)}, bf16[96,576]{1,0:T(8,128)(2,1)S(1)}, u32[]{:S(2)}, u32[]{:S(2)}) collective-permute-start(bf16[96,576]{1,0:T(8,128)(2,1)S(1)} %copy.217), channel_id=1, source_target_pairs={{0,1},{1,2},{2,3},{3,0},{4,5},{5,6},{6,7},{7,4},{8,9},{9,10},{10,1... | collective-permute-start | bytes 331784 | tf_op jit(solution)/shard_map/ppermute | solution.py:34
  45.8 9.0 %collective-permute-start.6 = (bf16[2,96,576]{2,1,0:T(8,128)(2,1)S(1)}, bf16[2,96,576]{2,1,0:T(8,128)(2,1)S(1)}, u32[]{:S(2)}, u32[]{:S(2)}) collective-permute-start(bf16[2,96,576]{2,1,0:T(8,128)(2,1)S(1)} %get-tuple-element.148), channel_id=1, source_target_pairs={{0,16},{4,20},{8,24},{12,28},{16,0},{20,4},{24,8},{28,12},{1,17},{... | collective-permute-start | bytes 663560 | tf_op jit(solution)/shard_map/ppermute | solution.py:30
  49.6 9.0 %collective-permute-start.1 = (bf16[2,96,576]{2,1,0:T(8,128)(2,1)S(1)}, bf16[2,96,576]{2,1,0:T(8,128)(2,1)S(1)}, u32[]{:S(2)}, u32[]{:S(2)}) collective-permute-start(bf16[2,96,576]{2,1,0:T(8,128)(2,1)S(1)} %get-tuple-element.145), channel_id=1, source_target_pairs={{0,8},{4,12},{8,0},{12,4},{16,24},{20,28},{24,16},{28,20},{1,9},{5... | collective-permute-start | bytes 663560 | tf_op jit(solution)/shard_map/ppermute | solution.py:30
  51.3 29.6 %collective-permute-start.21 = (bf16[2,216,768]{2,1,0:T(8,128)(2,1)S(1)}, bf16[2,216,768]{2,1,0:T(8,128)(2,1)S(1)}, u32[]{:S(2)}, u32[]{:S(2)}) collective-permute-start(bf16[2,216,768]{2,1,0:T(8,128)(2,1)S(1)} %get-tuple-element.131), channel_id=1, source_target_pairs={{0,16},{4,20},{8,24},{12,28},{16,0},{20,4},{24,8},{28,12},{1,17},{... | collective-permute-start | bytes 1990664 | tf_op jit(solution)/shard_map/ppermute | solution.py:30
  53.0 29.6 %collective-permute-start.16 = (bf16[2,216,768]{2,1,0:T(8,128)(2,1)S(1)}, bf16[2,216,768]{2,1,0:T(8,128)(2,1)S(1)}, u32[]{:S(2)}, u32[]{:S(2)}) collective-permute-start(bf16[2,216,768]{2,1,0:T(8,128)(2,1)S(1)} %get-tuple-element.128), channel_id=1, source_target_pairs={{0,8},{4,12},{8,0},{12,4},{16,24},{20,28},{24,16},{28,20},{1,9},{5... | collective-permute-start | bytes 1990664 | tf_op jit(solution)/shard_map/ppermute | solution.py:30
  54.9 24.1 %collective-permute-start.7 = (bf16[2,2,96,576]{3,2,1,0:T(8,128)(2,1)S(1)}, bf16[2,2,96,576]{3,2,1,0:T(8,128)(2,1)S(1)}, u32[]{:S(2)}, u32[]{:S(2)}) collective-permute-start(bf16[2,2,96,576]{3,2,1,0:T(8,128)(2,1)S(1)} %maximum_select_fusion.22), channel_id=1, source_target_pairs={{0,8},{4,12},{8,0},{12,4},{16,24},{20,28},{24,16},{28,20},{1,9},{5... | collective-permute-start | bytes 1327112 | tf_op jit(solution)/shard_map/ppermute | solution.py:30
  58.7 20.7 %collective-permute-start.2 = (bf16[2,2,96,576]{3,2,1,0:T(8,128)(2,1)S(1)}, bf16[2,2,96,576]{3,2,1,0:T(8,128)(2,1)S(1)}, u32[]{:S(2)}, u32[]{:S(2)}) collective-permute-start(bf16[2,2,96,576]{3,2,1,0:T(8,128)(2,1)S(1)} %maximum_select_fusion.20), channel_id=1, source_target_pairs={{0,16},{4,20},{8,24},{12,28},{16,0},{20,4},{24,8},{28,12},{1,17},{... | collective-permute-start | bytes 1327112 | tf_op jit(solution)/shard_map/ppermute | solution.py:30
  79.3 5.0 %collective-permute-start.8 = (bf16[2,2,2,96,576]{4,3,2,1,0:T(8,128)(2,1)S(1)}, bf16[2,2,2,96,576]{4,3,2,1,0:T(8,128)(2,1)S(1)}, u32[]{:S(2)}, u32[]{:S(2)}) collective-permute-start(bf16[2,2,2,96,576]{4,3,2,1,0:T(8,128)(2,1)S(1)} %maximum_select_fusion.14), channel_id=1, source_target_pairs={{0,4},{4,0},{8,12},{12,8},{16,20},{20,16},{24,28},{28,24},{1,5},{5... | collective-permute-start | bytes 2654216 | tf_op jit(solution)/shard_map/ppermute | solution.py:30
  79.6 5.2 %collective-permute-start.3 = (bf16[2,2,2,96,576]{4,3,2,0,1:T(8,128)(2,1)S(1)}, bf16[2,2,2,96,576]{4,3,2,0,1:T(8,128)(2,1)S(1)}, u32[]{:S(2)}, u32[]{:S(2)}) collective-permute-start(bf16[2,2,2,96,576]{4,3,2,0,1:T(8,128)(2,1)S(1)} %maximum_select_fusion.12), channel_id=1, source_target_pairs={{0,4},{4,0},{8,12},{12,8},{16,20},{20,16},{24,28},{28,24},{1,5},{5... | collective-permute-start | bytes 2654216 | tf_op jit(solution)/shard_map/ppermute | solution.py:30
  81.1 31.1 %collective-permute-start.22 = (bf16[2,2,216,768]{3,2,0,1:T(8,128)(2,1)S(1)}, bf16[2,2,216,768]{3,2,0,1:T(8,128)(2,1)S(1)}, u32[]{:S(2)}, u32[]{:S(2)}) collective-permute-start(bf16[2,2,216,768]{3,2,0,1:T(8,128)(2,1)S(1)} %maximum_select_fusion.9), channel_id=1, source_target_pairs={{0,8},{4,12},{8,0},{12,4},{16,24},{20,28},{24,16},{28,20},{1,9},{5... | collective-permute-start | bytes 3981320 | tf_op jit(solution)/shard_map/ppermute | solution.py:30
  82.8 31.7 %collective-permute-start.17 = (bf16[2,2,216,768]{3,2,1,0:T(8,128)(2,1)S(1)}, bf16[2,2,216,768]{3,2,1,0:T(8,128)(2,1)S(1)}, u32[]{:S(2)}, u32[]{:S(2)}) collective-permute-start(bf16[2,2,216,768]{3,2,1,0:T(8,128)(2,1)S(1)} %maximum_select_fusion.8), channel_id=1, source_target_pairs={{0,16},{4,20},{8,24},{12,28},{16,0},{20,4},{24,8},{28,12},{1,17},{... | collective-permute-start | bytes 3981320 | tf_op jit(solution)/shard_map/ppermute | solution.py:30
  91.2 23.2 %collective-permute-start.12 = (bf16[4,3,128,65]{2,3,1,0:T(8,128)(2,1)S(1)}, bf16[4,3,128,65]{2,3,1,0:T(8,128)(2,1)S(1)}, u32[]{:S(2)}, u32[]{:S(2)}) collective-permute-start(bf16[4,3,128,65]{2,3,1,0:T(8,128)(2,1)S(1)} %convolution_convert_fusion.1), channel_id=1, source_target_pairs={{0,1},{1,2},{2,3},{4,5},{5,6},{6,7},{8,9},{9,10},{10,11},{12,13},{... | collective-permute-start | bytes 599048 | tf_op jit(solution)/shard_map/ppermute | solution.py:39
  93.9 22.9 %collective-permute-start.13 = (bf16[4,3,128,65]{2,3,1,0:T(8,128)(2,1)S(1)}, bf16[4,3,128,65]{2,3,1,0:T(8,128)(2,1)S(1)}, u32[]{:S(2)}, u32[]{:S(2)}) collective-permute-start(bf16[4,3,128,65]{2,3,1,0:T(8,128)(2,1)S(1)} %convolution_convert_fusion.1), channel_id=1, source_target_pairs={{0,2},{1,3},{4,6},{5,7},{8,10},{9,11},{12,14},{13,15},{16,18},{17,... | collective-permute-start | bytes 599048 | tf_op jit(solution)/shard_map/ppermute | solution.py:39
  97.6 16.9 %collective-permute-start.14 = (bf16[4,3,128,65]{2,3,1,0:T(8,128)(2,1)S(1)}, bf16[4,3,128,65]{2,3,1,0:T(8,128)(2,1)S(1)}, u32[]{:S(2)}, u32[]{:S(2)}) collective-permute-start(bf16[4,3,128,65]{2,3,1,0:T(8,128)(2,1)S(1)} %convolution_convert_fusion.1), channel_id=1, source_target_pairs={{0,3},{4,7},{8,11},{12,15},{16,19},{20,23},{24,27},{28,31}} | collective-permute-start | bytes 599048 | tf_op jit(solution)/shard_map/ppermute | solution.py:39
  114.3 5.3 %collective-permute-start.23 = (bf16[2,2,2,216,768]{4,3,0,1,2:T(8,128)(2,1)}, bf16[2,2,2,216,768]{4,3,0,1,2:T(8,128)(2,1)}, u32[]{:S(2)}, u32[]{:S(2)}) collective-permute-start(bf16[2,2,2,216,768]{4,3,0,1,2:T(8,128)(2,1)} %maximum_select_fusion.4), channel_id=1, source_target_pairs={{0,4},{4,0},{8,12},{12,8},{16,20},{20,16},{24,28},{28,24},{1,5},{5... | collective-permute-start | bytes 7962632 | tf_op jit(solution)/shard_map/ppermute | solution.py:30
  116.3 6.9 %collective-permute-start.18 = (bf16[2,2,2,216,768]{4,3,2,1,0:T(8,128)(2,1)}, bf16[2,2,2,216,768]{4,3,2,1,0:T(8,128)(2,1)S(1)}, u32[]{:S(2)}, u32[]{:S(2)}) collective-permute-start(bf16[2,2,2,216,768]{4,3,2,1,0:T(8,128)(2,1)} %maximum_select_fusion.3), channel_id=1, source_target_pairs={{0,4},{4,0},{8,12},{12,8},{16,20},{20,16},{24,28},{28,24},{1,5},{5... | collective-permute-start | bytes 7962632 | tf_op jit(solution)/shard_map/ppermute | solution.py:30
  157.0 23.0 %copy-start.4 = (f32[512,768]{1,0:T(8,128)}, f32[512,768]{1,0:T(8,128)S(1)}, u32[]{:S(2)}) copy-start(f32[512,768]{1,0:T(8,128)S(1)} %get-tuple-element.99) | copy-start | bytes 4718596
  160.6 31.5 %collective-permute-start.24 = (bf16[4,3,128,65]{2,3,1,0:T(8,128)(2,1)}, bf16[4,3,128,65]{2,3,1,0:T(8,128)(2,1)}, u32[]{:S(2)}, u32[]{:S(2)}) collective-permute-start(bf16[4,3,128,65]{2,3,1,0:T(8,128)(2,1)} %convolution_convert_fusion), channel_id=1, source_target_pairs={{1,0},{2,1},{3,2},{5,4},{6,5},{7,6},{9,8},{10,9},{11,10},{13,12},{... | collective-permute-start | bytes 599048 | tf_op jit(solution)/shard_map/ppermute | solution.py:39
  162.2 33.6 %collective-permute-start.25 = (bf16[4,3,128,65]{2,3,1,0:T(8,128)(2,1)}, bf16[4,3,128,65]{2,3,1,0:T(8,128)(2,1)}, u32[]{:S(2)}, u32[]{:S(2)}) collective-permute-start(bf16[4,3,128,65]{2,3,1,0:T(8,128)(2,1)} %convolution_convert_fusion), channel_id=1, source_target_pairs={{2,0},{3,1},{6,4},{7,5},{10,8},{11,9},{14,12},{15,13},{18,16},{19,... | collective-permute-start | bytes 599048 | tf_op jit(solution)/shard_map/ppermute | solution.py:39
  163.5 30.5 %collective-permute-start.26 = (bf16[4,3,128,65]{2,3,1,0:T(8,128)(2,1)}, bf16[4,3,128,65]{2,3,1,0:T(8,128)(2,1)}, u32[]{:S(2)}, u32[]{:S(2)}) collective-permute-start(bf16[4,3,128,65]{2,3,1,0:T(8,128)(2,1)} %convolution_convert_fusion), channel_id=1, source_target_pairs={{3,0},{7,4},{11,8},{15,12},{19,16},{23,20},{27,24},{31,28}} | collective-permute-start | bytes 599048 | tf_op jit(solution)/shard_map/ppermute | solution.py:39
  183.6 36.5 %collective-permute-start.36 = (bf16[4,2,2,24,768]{4,3,2,1,0:T(8,128)(2,1)}, bf16[4,2,2,24,768]{4,3,2,1,0:T(8,128)(2,1)}, u32[]{:S(2)}, u32[]{:S(2)}) collective-permute-start(bf16[4,2,2,24,768]{4,3,2,1,0:T(8,128)(2,1)} %fusion.68), channel_id=1, source_target_pairs={{0,4},{4,0},{8,12},{12,8},{16,20},{20,16},{24,28},{28,24},{1,5},{5... | collective-permute-start | bytes 1769480 | tf_op jit(solution)/shard_map/ppermute | solution.py:30
  187.9 108.4 %collective-permute-start.45 = (bf16[4,2,2,96,768]{4,3,0,2,1:T(8,128)(2,1)}, bf16[4,2,2,96,768]{4,3,0,2,1:T(8,128)(2,1)}, u32[]{:S(2)}, u32[]{:S(2)}) collective-permute-start(bf16[4,2,2,96,768]{4,3,0,2,1:T(8,128)(2,1)} %fusion.8), channel_id=1, source_target_pairs={{0,4},{4,0},{8,12},{12,8},{16,20},{20,16},{24,28},{28,24},{1,5},{5... | collective-permute-start | bytes 7077896 | tf_op jit(solution)/shard_map/ppermute | solution.py:30
  221.4 9.1 %collective-permute-start.37 = (bf16[4,2,24,768]{3,2,1,0:T(8,128)(2,1)S(1)}, bf16[4,2,24,768]{3,2,1,0:T(8,128)(2,1)S(1)}, u32[]{:S(2)}, u32[]{:S(2)}) collective-permute-start(bf16[4,2,24,768]{3,2,1,0:T(8,128)(2,1)S(1)} %fusion.74), channel_id=1, source_target_pairs={{0,8},{4,12},{8,0},{12,4},{16,24},{20,28},{24,16},{28,20},{1,9},{5... | collective-permute-start | bytes 884744 | tf_op jit(solution)/shard_map/ppermute | solution.py:30
  226.5 63.3 %collective-permute-start.27 = (bf16[4,2,2,96,576]{4,3,2,1,0:T(8,128)(2,1)}, bf16[4,2,2,96,576]{4,3,2,1,0:T(8,128)(2,1)}, u32[]{:S(2)}, u32[]{:S(2)}) collective-permute-start(bf16[4,2,2,96,576]{4,3,2,1,0:T(8,128)(2,1)} %fusion.13), channel_id=1, source_target_pairs={{0,4},{4,0},{8,12},{12,8},{16,20},{20,16},{24,28},{28,24},{1,5},{5... | collective-permute-start | bytes 5308424 | tf_op jit(solution)/shard_map/ppermute | solution.py:30
  230.6 5.2 %collective-permute-start.38 = (bf16[4,24,768]{2,1,0:T(8,128)(2,1)S(1)}, bf16[4,24,768]{2,1,0:T(8,128)(2,1)S(1)}, u32[]{:S(2)}, u32[]{:S(2)}) collective-permute-start(bf16[4,24,768]{2,1,0:T(8,128)(2,1)S(1)} %fusion.88), channel_id=1, source_target_pairs={{0,16},{4,20},{8,24},{12,28},{16,0},{20,4},{24,8},{28,12},{1,17},{... | collective-permute-start | bytes 442376 | tf_op jit(solution)/shard_map/ppermute | solution.py:30
  235.8 47.6 %collective-permute-start.41 = (bf16[24,768]{1,0:T(8,128)(2,1)S(1)}, bf16[24,768]{1,0:T(8,128)(2,1)S(1)}, u32[]{:S(2)}, u32[]{:S(2)}) collective-permute-start(bf16[24,768]{1,0:T(8,128)(2,1)S(1)} %get-tuple-element.154), channel_id=1, source_target_pairs={{0,1},{1,2},{2,3},{3,0},{4,5},{5,6},{6,7},{7,4},{8,9},{9,10},{10,1... | collective-permute-start | bytes 110600 | tf_op jit(solution)/shard_map/ppermute | solution.py:34
  238.4 45.1 %collective-permute-start.40 = (bf16[24,768]{1,0:T(8,128)(2,1)S(1)}, bf16[24,768]{1,0:T(8,128)(2,1)S(1)}, u32[]{:S(2)}, u32[]{:S(2)}) collective-permute-start(bf16[24,768]{1,0:T(8,128)(2,1)S(1)} %get-tuple-element.155), channel_id=1, source_target_pairs={{0,2},{1,3},{2,0},{3,1},{4,6},{5,7},{6,4},{7,5},{8,10},{9,11},{10,... | collective-permute-start | bytes 110600 | tf_op jit(solution)/shard_map/ppermute | solution.py:34
  243.3 40.2 %collective-permute-start.39 = (bf16[24,768]{1,0:T(8,128)(2,1)S(1)}, bf16[24,768]{1,0:T(8,128)(2,1)S(1)}, u32[]{:S(2)}, u32[]{:S(2)}) collective-permute-start(bf16[24,768]{1,0:T(8,128)(2,1)S(1)} %get-tuple-element.153), channel_id=1, source_target_pairs={{0,3},{1,0},{2,1},{3,2},{4,7},{5,4},{6,5},{7,6},{8,11},{9,8},{10,9... | collective-permute-start | bytes 110600 | tf_op jit(solution)/shard_map/ppermute | solution.py:34
  283.4 35.1 %collective-permute-start.54 = (bf16[4,2,2,96,768]{4,3,0,2,1:T(8,128)(2,1)}, bf16[4,2,2,96,768]{4,3,0,2,1:T(8,128)(2,1)S(1)}, u32[]{:S(2)}, u32[]{:S(2)}) collective-permute-start(bf16[4,2,2,96,768]{4,3,0,2,1:T(8,128)(2,1)} %fusion.9), channel_id=1, source_target_pairs={{0,4},{4,0},{8,12},{12,8},{16,20},{20,16},{24,28},{28,24},{1,5},{5... | collective-permute-start | bytes 7077896 | tf_op jit(solution)/shard_map/ppermute | solution.py:30
  283.5 4.5 %collective-permute-start.42 = (bf16[24,768]{1,0:T(8,128)(2,1)S(1)}, bf16[24,768]{1,0:T(8,128)(2,1)S(1)}, u32[]{:S(2)}, u32[]{:S(2)}) collective-permute-start(bf16[24,768]{1,0:T(8,128)(2,1)S(1)} %fusion.92), channel_id=1, source_target_pairs={{0,16},{4,20},{8,24},{12,28},{16,0},{20,4},{24,8},{28,12},{1,17},{... | collective-permute-start | bytes 110600 | tf_op jit(solution)/shard_map/ppermute | solution.py:30
  288.0 6.7 %collective-permute-start.43 = (bf16[2,24,768]{2,1,0:T(8,128)(2,1)S(1)}, bf16[2,24,768]{2,1,0:T(8,128)(2,1)S(1)}, u32[]{:S(2)}, u32[]{:S(2)}) collective-permute-start(bf16[2,24,768]{2,1,0:T(8,128)(2,1)S(1)} %maximum_select_fusion.35), channel_id=1, source_target_pairs={{0,8},{4,12},{8,0},{12,4},{16,24},{20,28},{24,16},{28,20},{1,9},{5... | collective-permute-start | bytes 221192 | tf_op jit(solution)/shard_map/ppermute | solution.py:30
  293.1 23.3 %collective-permute-start.28 = (bf16[4,2,96,576]{3,2,1,0:T(8,128)(2,1)S(1)}, bf16[4,2,96,576]{3,2,1,0:T(8,128)(2,1)S(1)}, u32[]{:S(2)}, u32[]{:S(2)}) collective-permute-start(bf16[4,2,96,576]{3,2,1,0:T(8,128)(2,1)S(1)} %fusion.43), channel_id=1, source_target_pairs={{0,16},{4,20},{8,24},{12,28},{16,0},{20,4},{24,8},{28,12},{1,17},{... | collective-permute-start | bytes 2654216 | tf_op jit(solution)/shard_map/ppermute | solution.py:30
  294.8 1.4 collective-permute-start.44
  316.6 11.8 %collective-permute-start.29 = (bf16[4,96,576]{2,1,0:T(8,128)(2,1)S(1)}, bf16[4,96,576]{2,1,0:T(8,128)(2,1)S(1)}, u32[]{:S(2)}, u32[]{:S(2)}) collective-permute-start(bf16[4,96,576]{2,1,0:T(8,128)(2,1)S(1)} %fusion.72), channel_id=1, source_target_pairs={{0,8},{4,12},{8,0},{12,4},{16,24},{20,28},{24,16},{28,20},{1,9},{5... | collective-permute-start | bytes 1327112 | tf_op jit(solution)/shard_map/ppermute | solution.py:30
  317.3 43.7 %collective-permute-start.46 = (bf16[4,2,96,768]{3,2,0,1:T(8,128)(2,1)S(1)}, bf16[4,2,96,768]{3,2,0,1:T(8,128)(2,1)S(1)}, u32[]{:S(2)}, u32[]{:S(2)}) collective-permute-start(bf16[4,2,96,768]{3,2,0,1:T(8,128)(2,1)S(1)} %fusion.40), channel_id=1, source_target_pairs={{0,16},{4,20},{8,24},{12,28},{16,0},{20,4},{24,8},{28,12},{1,17},{... | collective-permute-start | bytes 3538952 | tf_op jit(solution)/shard_map/ppermute | solution.py:30
  328.6 7.6 %collective-permute-start.32 = (bf16[96,576]{1,0:T(8,128)(2,1)S(1)}, bf16[96,576]{1,0:T(8,128)(2,1)S(1)}, u32[]{:S(2)}, u32[]{:S(2)}) collective-permute-start(bf16[96,576]{1,0:T(8,128)(2,1)S(1)} %get-tuple-element.139), channel_id=1, source_target_pairs={{0,1},{1,2},{2,3},{3,0},{4,5},{5,6},{6,7},{7,4},{8,9},{9,10},{10,1... | collective-permute-start | bytes 331784 | tf_op jit(solution)/shard_map/ppermute | solution.py:34
  328.7 10.1 %collective-permute-start.31 = (bf16[96,576]{1,0:T(8,128)(2,1)S(1)}, bf16[96,576]{1,0:T(8,128)(2,1)S(1)}, u32[]{:S(2)}, u32[]{:S(2)}) collective-permute-start(bf16[96,576]{1,0:T(8,128)(2,1)S(1)} %get-tuple-element.140), channel_id=1, source_target_pairs={{0,2},{1,3},{2,0},{3,1},{4,6},{5,7},{6,4},{7,5},{8,10},{9,11},{10,... | collective-permute-start | bytes 331784 | tf_op jit(solution)/shard_map/ppermute | solution.py:34
  330.8 8.0 %collective-permute-start.30 = (bf16[96,576]{1,0:T(8,128)(2,1)S(1)}, bf16[96,576]{1,0:T(8,128)(2,1)S(1)}, u32[]{:S(2)}, u32[]{:S(2)}) collective-permute-start(bf16[96,576]{1,0:T(8,128)(2,1)S(1)} %get-tuple-element.138), channel_id=1, source_target_pairs={{0,3},{1,0},{2,1},{3,2},{4,7},{5,4},{6,5},{7,6},{8,11},{9,8},{10,9... | collective-permute-start | bytes 331784 | tf_op jit(solution)/shard_map/ppermute | solution.py:34
  332.6 29.7 %collective-permute-start.55 = (bf16[4,2,96,768]{3,2,0,1:T(8,128)(2,1)S(1)}, bf16[4,2,96,768]{3,2,0,1:T(8,128)(2,1)S(1)}, u32[]{:S(2)}, u32[]{:S(2)}) collective-permute-start(bf16[4,2,96,768]{3,2,0,1:T(8,128)(2,1)S(1)} %fusion.41), channel_id=1, source_target_pairs={{0,8},{4,12},{8,0},{12,4},{16,24},{20,28},{24,16},{28,20},{1,9},{5... | collective-permute-start | bytes 3538952 | tf_op jit(solution)/shard_map/ppermute | solution.py:30
  338.9 21.9 %collective-permute-start.33 = (bf16[96,576]{1,0:T(8,128)(2,1)S(1)}, bf16[96,576]{1,0:T(8,128)(2,1)S(1)}, u32[]{:S(2)}, u32[]{:S(2)}) collective-permute-start(bf16[96,576]{1,0:T(8,128)(2,1)S(1)} %fusion.86), channel_id=1, source_target_pairs={{0,8},{4,12},{8,0},{12,4},{16,24},{20,28},{24,16},{28,20},{1,9},{5... | collective-permute-start | bytes 331784 | tf_op jit(solution)/shard_map/ppermute | solution.py:30
  360.8 9.0 %collective-permute-start.34 = (bf16[2,96,576]{2,1,0:T(8,128)(2,1)S(1)}, bf16[2,96,576]{2,1,0:T(8,128)(2,1)S(1)}, u32[]{:S(2)}, u32[]{:S(2)}) collective-permute-start(bf16[2,96,576]{2,1,0:T(8,128)(2,1)S(1)} %maximum_select_fusion.31), channel_id=1, source_target_pairs={{0,16},{4,20},{8,24},{12,28},{16,0},{20,4},{24,8},{28,12},{1,17},{... | collective-permute-start | bytes 663560 | tf_op jit(solution)/shard_map/ppermute | solution.py:30
  361.4 11.6 %collective-permute-start.47 = (bf16[4,96,768]{2,1,0:T(8,128)(2,1)S(1)}, bf16[4,96,768]{2,1,0:T(8,128)(2,1)S(1)}, u32[]{:S(2)}, u32[]{:S(2)}) collective-permute-start(bf16[4,96,768]{2,1,0:T(8,128)(2,1)S(1)} %fusion.69), channel_id=1, source_target_pairs={{0,8},{4,12},{8,0},{12,4},{16,24},{20,28},{24,16},{28,20},{1,9},{5... | collective-permute-start | bytes 1769480 | tf_op jit(solution)/shard_map/ppermute | solution.py:30
  362.6 15.3 %collective-permute-start.56 = (bf16[4,96,768]{2,1,0:T(8,128)(2,1)S(1)}, bf16[4,96,768]{2,1,0:T(8,128)(2,1)S(1)}, u32[]{:S(2)}, u32[]{:S(2)}) collective-permute-start(bf16[4,96,768]{2,1,0:T(8,128)(2,1)S(1)} %fusion.70), channel_id=1, source_target_pairs={{0,16},{4,20},{8,24},{12,28},{16,0},{20,4},{24,8},{28,12},{1,17},{... | collective-permute-start | bytes 1769480 | tf_op jit(solution)/shard_map/ppermute | solution.py:30
  369.9 8.2 %collective-permute-start.35 = (bf16[2,2,96,576]{3,2,1,0:T(8,128)(2,1)S(1)}, bf16[2,2,96,576]{3,2,1,0:T(8,128)(2,1)S(1)}, u32[]{:S(2)}, u32[]{:S(2)}) collective-permute-start(bf16[2,2,96,576]{3,2,1,0:T(8,128)(2,1)S(1)} %maximum_select_fusion.24), channel_id=1, source_target_pairs={{0,4},{4,0},{8,12},{12,8},{16,20},{20,16},{24,28},{28,24},{1,5},{5... | collective-permute-start | bytes 1327112 | tf_op jit(solution)/shard_map/ppermute | solution.py:30
  373.1 8.7 %collective-permute-start.50 = (bf16[96,768]{1,0:T(8,128)(2,1)S(1)}, bf16[96,768]{1,0:T(8,128)(2,1)S(1)}, u32[]{:S(2)}, u32[]{:S(2)}) collective-permute-start(bf16[96,768]{1,0:T(8,128)(2,1)S(1)} %get-tuple-element.136), channel_id=1, source_target_pairs={{0,1},{1,2},{2,3},{3,0},{4,5},{5,6},{6,7},{7,4},{8,9},{9,10},{10,1... | collective-permute-start | bytes 442376 | tf_op jit(solution)/shard_map/ppermute | solution.py:34
  373.8 14.3 %collective-permute-start.49 = (bf16[96,768]{1,0:T(8,128)(2,1)S(1)}, bf16[96,768]{1,0:T(8,128)(2,1)S(1)}, u32[]{:S(2)}, u32[]{:S(2)}) collective-permute-start(bf16[96,768]{1,0:T(8,128)(2,1)S(1)} %get-tuple-element.137), channel_id=1, source_target_pairs={{0,2},{1,3},{2,0},{3,1},{4,6},{5,7},{6,4},{7,5},{8,10},{9,11},{10,... | collective-permute-start | bytes 442376 | tf_op jit(solution)/shard_map/ppermute | solution.py:34
  375.0 13.1 %collective-permute-start.48 = (bf16[96,768]{1,0:T(8,128)(2,1)S(1)}, bf16[96,768]{1,0:T(8,128)(2,1)S(1)}, u32[]{:S(2)}, u32[]{:S(2)}) collective-permute-start(bf16[96,768]{1,0:T(8,128)(2,1)S(1)} %get-tuple-element.135), channel_id=1, source_target_pairs={{0,3},{1,0},{2,1},{3,2},{4,7},{5,4},{6,5},{7,6},{8,11},{9,8},{10,9... | collective-permute-start | bytes 442376 | tf_op jit(solution)/shard_map/ppermute | solution.py:34
  378.1 13.1 %collective-permute-start.59 = (bf16[96,768]{1,0:T(8,128)(2,1)S(1)}, bf16[96,768]{1,0:T(8,128)(2,1)S(1)}, u32[]{:S(2)}, u32[]{:S(2)}) collective-permute-start(bf16[96,768]{1,0:T(8,128)(2,1)S(1)} %get-tuple-element.133), channel_id=1, source_target_pairs={{0,1},{1,2},{2,3},{3,0},{4,5},{5,6},{6,7},{7,4},{8,9},{9,10},{10,1... | collective-permute-start | bytes 442376 | tf_op jit(solution)/shard_map/ppermute | solution.py:34
  378.1 19.4 %collective-permute-start.58 = (bf16[96,768]{1,0:T(8,128)(2,1)S(1)}, bf16[96,768]{1,0:T(8,128)(2,1)S(1)}, u32[]{:S(2)}, u32[]{:S(2)}) collective-permute-start(bf16[96,768]{1,0:T(8,128)(2,1)S(1)} %get-tuple-element.134), channel_id=1, source_target_pairs={{0,2},{1,3},{2,0},{3,1},{4,6},{5,7},{6,4},{7,5},{8,10},{9,11},{10,... | collective-permute-start | bytes 442376 | tf_op jit(solution)/shard_map/ppermute | solution.py:34
  381.8 15.7 %collective-permute-start.57 = (bf16[96,768]{1,0:T(8,128)(2,1)S(1)}, bf16[96,768]{1,0:T(8,128)(2,1)S(1)}, u32[]{:S(2)}, u32[]{:S(2)}) collective-permute-start(bf16[96,768]{1,0:T(8,128)(2,1)S(1)} %get-tuple-element.132), channel_id=1, source_target_pairs={{0,3},{1,0},{2,1},{3,2},{4,7},{5,4},{6,5},{7,6},{8,11},{9,8},{10,9... | collective-permute-start | bytes 442376 | tf_op jit(solution)/shard_map/ppermute | solution.py:34
  388.2 12.5 %collective-permute-start.51 = (bf16[96,768]{1,0:T(8,128)(2,1)S(1)}, bf16[96,768]{1,0:T(8,128)(2,1)S(1)}, u32[]{:S(2)}, u32[]{:S(2)}) collective-permute-start(bf16[96,768]{1,0:T(8,128)(2,1)S(1)} %fusion.82), channel_id=1, source_target_pairs={{0,8},{4,12},{8,0},{12,4},{16,24},{20,28},{24,16},{28,20},{1,9},{5... | collective-permute-start | bytes 442376 | tf_op jit(solution)/shard_map/ppermute | solution.py:30
  397.7 6.8 %collective-permute-start.60 = (bf16[96,768]{1,0:T(8,128)(2,1)S(1)}, bf16[96,768]{1,0:T(8,128)(2,1)S(1)}, u32[]{:S(2)}, u32[]{:S(2)}) collective-permute-start(bf16[96,768]{1,0:T(8,128)(2,1)S(1)} %fusion.78), channel_id=1, source_target_pairs={{0,16},{4,20},{8,24},{12,28},{16,0},{20,4},{24,8},{28,12},{1,17},{... | collective-permute-start | bytes 442376 | tf_op jit(solution)/shard_map/ppermute | solution.py:30
  400.7 8.3 %collective-permute-start.52 = (bf16[2,96,768]{2,1,0:T(8,128)(2,1)S(1)}, bf16[2,96,768]{2,1,0:T(8,128)(2,1)S(1)}, u32[]{:S(2)}, u32[]{:S(2)}) collective-permute-start(bf16[2,96,768]{2,1,0:T(8,128)(2,1)S(1)} %maximum_select_fusion.27), channel_id=1, source_target_pairs={{0,16},{4,20},{8,24},{12,28},{16,0},{20,4},{24,8},{28,12},{1,17},{... | collective-permute-start | bytes 884744 | tf_op jit(solution)/shard_map/ppermute | solution.py:30
  404.5 6.8 %collective-permute-start.61 = (bf16[2,96,768]{2,1,0:T(8,128)(2,1)S(1)}, bf16[2,96,768]{2,1,0:T(8,128)(2,1)S(1)}, u32[]{:S(2)}, u32[]{:S(2)}) collective-permute-start(bf16[2,96,768]{2,1,0:T(8,128)(2,1)S(1)} %maximum_select_fusion.29), channel_id=1, source_target_pairs={{0,8},{4,12},{8,0},{12,4},{16,24},{20,28},{24,16},{28,20},{1,9},{5... | collective-permute-start | bytes 884744 | tf_op jit(solution)/shard_map/ppermute | solution.py:30
  409.2 2.5 collective-permute-start.53
  411.4 2.1 collective-permute-start.62
  (28 other events, 291.0 us)
